TPU v7x, 128 devices: a whole 4x4x4 slice. The times are simulated.
128 devices in a mesh: site: 8 (over z, core), bond: 16 (over y, x).
Axes of the slice: x: 4, y: 4, z: 4, core: 2. Of those that a mesh axis runs over, the one named last changes fastest.
Arguments:
- left_env: float32 [8, 512, 16, 512], P('site', 'bond'), may hold values from -6 to 6
- right_env: float32 [8, 512, 16, 512], P('site', 'bond'), may hold values from -6 to 6
- left_site: float32 [8, 512, 4, 512], P('site'), may hold values from -0.125 to 0.125
- right_site: float32 [8, 512, 4, 512], P('site'), may hold values from -0.125 to 0.125
- left_mpo: float32 [8, 16, 16, 4, 4], P('site'), may hold values from -1.5 to 1.5
- right_mpo: float32 [8, 16, 16, 4, 4], P('site'), may hold values from -1.5 to 1.5
Outputs:
- new_left: float32 [8, 512, 16, 512], P('site', 'bond')
- new_right: float32 [8, 512, 16, 512], P('site', 'bond')
All inputs are finite; a program needn't handle non-finite values.
Results may differ from a plain program's by a relative error of at most 0.0001.
Values sent between devices are 32-bit elements; how exact they have to be, the bound alone decides.
A program may use at most 128 MiB of HBM per device.

v0:
```python
import jax
import jax.numpy as jnp
from jax import lax
from jax.sharding import PartitionSpec as P


def passed_along(block, axis, distance):
    devices = range(lax.axis_size(axis))
    route = [(i - distance, i) for i in devices if i - distance in devices]
    return lax.ppermute(block, axis, route)


def finish_env(first_part, tensor, operator, rows_dev):
    depth = tensor.shape[0]
    states = tensor.shape[1]
    width = operator.shape[0]
    shaped = first_part.reshape(width, depth, states, rows_dev)
    second_part = jnp.einsum("wcsb,wvst->bvct", shaped, operator, precision=lax.Precision.HIGHEST)
    result = jnp.dot(
        second_part.reshape(rows_dev * width, depth * states),
        tensor.reshape(depth * states, depth),
        precision=lax.Precision.HIGHEST,
    )
    return result.reshape(rows_dev, width, depth)


def grow_rows(environ, tensor, position):
    rows_dev = environ.shape[0]
    width = environ.shape[1]
    depth = environ.shape[2]
    states = tensor.shape[1]
    columns = lax.dynamic_slice_in_dim(tensor, position * rows_dev, rows_dev, 2).reshape(
        depth, states * rows_dev
    )

    def add_piece(carry, piece, start):
        count = piece.shape[0]
        return lax.dot_general(
            piece.reshape(count, width * depth),
            columns,
            (((0,), (0,)), ((), ())),
            precision=lax.Precision.HIGHEST,
        )

    return (add_piece, jnp.zeros((width * depth, states * rows_dev), jnp.float32))


def local(left_env, right_env, left_site, right_site, left_mpo, right_mpo):
    position = lax.axis_index("bond")
    left_environ = left_env[0]
    right_environ = right_env[0]
    left_tensor = left_site[0]
    right_tensor = right_site[0]
    left_operator = left_mpo[0]
    right_operator = jnp.transpose(right_mpo[0], (1, 0, 2, 3))
    rows_dev = left_environ.shape[0]
    add_left, zero_left = grow_rows(left_environ, left_tensor, position)
    left_first = add_left(
        zero_left, lax.all_gather(left_environ, "bond", axis=0, tiled=True), jnp.int32(0)
    )
    grown_left = finish_env(left_first, left_tensor, left_operator, rows_dev)
    add_right, zero_right = grow_rows(right_environ, right_tensor, position)
    right_first = add_right(
        zero_right, lax.all_gather(right_environ, "bond", axis=0, tiled=True), jnp.int32(0)
    )
    grown_right = finish_env(right_first, right_tensor, right_operator, rows_dev)
    segment = lax.axis_index("site")
    last_segment = lax.axis_size("site") - 1
    from_left = passed_along(grown_left, "site", 1)
    from_right = passed_along(grown_right, "site", -1)
    new_left = jnp.where(segment == 0, left_environ, from_left)
    new_right = jnp.where(segment == last_segment, right_environ, from_right)
    return (new_left[None], new_right[None])


def solution(mesh):
    return jax.shard_map(
        local,
        mesh=mesh,
        in_specs=(
            P("site", "bond", None, None),
            P("site", "bond", None, None),
            P("site", None, None, None),
            P("site", None, None, None),
            P("site", None, None, None, None),
            P("site", None, None, None, None),
        ),
        out_specs=(P("site", "bond", None, None), P("site", "bond", None, None)),
        check_vma=False,
    )
```

profile of v0, /device:TPU:1, one launch (start us, length us, event | category | flops | bytes accessed | tf_op | source)
XLA Modules:
  0.0 338.0 jit_solution(9617925010033270167)
XLA Ops:
  7.2 0.0 all-gather.5.cloned.1.call-start
  7.2 0.7 all-gather.5.cloned.1.call-update
  7.9 0.0 all-gather.7.cloned.1.call-start
  7.9 0.7 all-gather.7.cloned.1.call-update
  8.7 5.3 %reshape.47 = f32[2048,512,1]{1,0,2:T(8,128)} reshape(f32[1,512,4,512]{3,2,1,0:T(4,128)} %param.8) | data formatting | bytes 8388608 | tf_op jit(solution)/shard_map/reshape;squeeze | solution.py:21
  14.0 5.3 %reshape.51 = f32[2048,512,1]{1,0,2:T(8,128)} reshape(f32[1,512,4,512]{3,2,1,0:T(4,128)} %param.9) | data formatting | bytes 8388608 | tf_op jit(solution)/shard_map/reshape;squeeze | solution.py:21
  19.3 0.0 copy-start.3
  19.3 2.7 constant_dynamic-slice_fusion
  22.1 0.3 copy.42
  22.4 0.0 copy-done.3
  22.4 0.1 copy.25
  22.5 0.3 copy.43
  22.9 101.4 %all-gather.5.cloned.1.call-done = f32[1,512,16,512]{3,2,0,1:T(8,128)} async-done(((f32[1,32,16,512]{3,2,0,1:T(8,128)}), f32[1,512,16,512]{3,2,0,1:T(8,128)}) %all-gather.5.cloned.1.call-update) | async-done | bytes 16777232 | tf_op jit(solution)/shard_map/all_gather | solution.py:59
  124.2 19.6 %copy.44 = f32[64,8,16,512]{3,1,2,0:T(8,128)S(1)} copy(f32[64,8,16,512]{3,2,1,0:T(8,128)} %bitcast.75) | data formatting | bytes 33554432
  143.8 9.1 %fusion.15 = f32[128,8192]{1,0:T(8,128)S(1)} fusion(f32[512,128]{0,1:T(8,128)S(1)} %bitcast.83, f32[512,8192]{1,0:T(8,128)S(1)} %bitcast.72), kind=kOutput, calls=%fused_computation.15 | convolution fusion | flops 6442450944 | bytes 21233664 | tf_op jit(solution)/shard_map/dot_general | solution.py:38
  153.0 3.4 %copy.45 = f32[16,8,16,512]{3,2,1,0:T(8,128)S(1)} copy(f32[16,8,16,512]{3,1,2,0:T(8,128)S(1)} %bitcast.78) | data formatting | bytes 8388608
  156.4 5.4 %fusion.4 = f32[32,16,512,4]{2,1,3,0:T(8,128)} fusion(f32[16,512,4,32,1]{1,0,3,2,4:T(8,128)S(1)} %bitcast.76, f32[16,16,4,4]{0,1,2,3:T(8,128)S(1)} %copy.25), kind=kOutput, calls=%fused_computation.4 | convolution fusion | flops 805306368 | bytes 8404992 | tf_op jit(solution)/shard_map/wcsb,wvst->bvct/dot_general | solution.py:18
  161.8 14.6 %copy.26 = f32[32,16,512,4]{0,1,3,2:T(8,128)} copy(f32[32,16,512,4]{2,1,3,0:T(8,128)} %fusion.4) | data formatting | bytes 8388608 | tf_op jit(solution)/shard_map/wcsb,wvst->bvct/transpose | solution.py:18
  176.3 12.2 %copy.27 = f32[32,16,2048]{2,1,0:T(8,128)} copy(f32[32,16,2048]{0,1,2:T(8,128)} %bitcast.70) | data formatting | bytes 8388608 | tf_op jit(solution)/shard_map/dot_general | solution.py:19
  188.5 9.4 %fusion.16 = f32[32,16,512]{2,1,0:T(8,128)S(1)} fusion(f32[32,16,2048]{2,1,0:T(8,128)} %copy.27, f32[2048,512,1]{1,0,2:T(8,128)} %reshape.47), kind=kOutput, calls=%fused_computation.16 | convolution fusion | flops 6442450944 | bytes 9437184 | tf_op jit(solution)/shard_map/dot_general | solution.py:19
  197.9 3.9 %collective-permute-start = (f32[32,16,512]{2,1,0:T(8,128)S(1)}, f32[32,16,512]{2,1,0:T(8,128)}, u32[]{:S(2)}, u32[]{:S(2)}) collective-permute-start(f32[32,16,512]{2,1,0:T(8,128)S(1)} %fusion.16), channel_id=1, source_target_pairs={{0,16},{16,32},{32,48},{48,64},{64,80},{80,96},{96,112},{1,17},{17... | collective-permute-start | bytes 3145736 | tf_op jit(solution)/shard_map/ppermute | solution.py:10
  201.9 35.3 %all-gather.7.cloned.1.call-done = f32[1,512,16,512]{3,2,0,1:T(8,128)} async-done(((f32[1,32,16,512]{3,2,0,1:T(8,128)}), f32[1,512,16,512]{3,2,0,1:T(8,128)}) %all-gather.7.cloned.1.call-update) | async-done | bytes 16777232 | tf_op jit(solution)/shard_map/all_gather | solution.py:64
  237.2 19.3 %copy.46 = f32[64,8,16,512]{3,1,2,0:T(8,128)S(1)} copy(f32[64,8,16,512]{3,2,1,0:T(8,128)} %bitcast.74) | data formatting | bytes 33554432
  256.5 9.1 %fusion.17 = f32[128,8192]{1,0:T(8,128)S(1)} fusion(f32[512,128]{0,1:T(8,128)S(1)} %bitcast.82, f32[512,8192]{1,0:T(8,128)S(1)} %bitcast.73), kind=kOutput, calls=%fused_computation.17 | convolution fusion | flops 6442450944 | bytes 21233664 | tf_op jit(solution)/shard_map/dot_general | solution.py:38
  265.7 0.0 copy-start.2
  265.7 3.5 %copy.47 = f32[16,8,16,512]{3,2,1,0:T(8,128)S(1)} copy(f32[16,8,16,512]{3,1,2,0:T(8,128)S(1)} %bitcast.79) | data formatting | bytes 8388608
  269.2 0.0 copy-done.2
  269.2 5.5 %fusion.7 = f32[32,16,512,4]{2,1,3,0:T(8,128)} fusion(f32[16,512,4,32,1]{1,0,3,2,4:T(8,128)S(1)} %bitcast.77, f32[16,16,4,4]{0,3,2,1:T(4,128)S(1)} %bitcast.84), kind=kOutput, calls=%fused_computation.5 | convolution fusion | flops 805306368 | bytes 8404992 | tf_op jit(solution)/shard_map/wcsb,wvst->bvct/dot_general | solution.py:18
  274.7 14.6 %copy.32 = f32[32,16,512,4]{0,1,3,2:T(8,128)} copy(f32[32,16,512,4]{2,1,3,0:T(8,128)} %fusion.7) | data formatting | bytes 8388608 | tf_op jit(solution)/shard_map/wcsb,wvst->bvct/transpose | solution.py:18
  289.2 12.0 %copy.33 = f32[32,16,2048]{2,1,0:T(8,128)} copy(f32[32,16,2048]{0,1,2:T(8,128)} %bitcast.71) | data formatting | bytes 8388608 | tf_op jit(solution)/shard_map/dot_general | solution.py:19
  301.2 0.0 copy-start
  301.2 0.0 copy-start.1
  301.2 10.4 %fusion.18 = f32[32,16,512]{2,1,0:T(8,128)} fusion(f32[32,16,2048]{2,1,0:T(8,128)} %copy.33, f32[2048,512,1]{1,0,2:T(8,128)} %reshape.51), kind=kOutput, calls=%fused_computation.18 | convolution fusion | flops 6442450944 | bytes 9437184 | tf_op jit(solution)/shard_map/dot_general | solution.py:19
  311.6 2.7 collective-permute-start.1
  314.3 0.0 collective-permute-done
  314.4 0.0 copy-done
  314.4 2.4 fusion.11
  316.8 11.5 %collective-permute-done.1 = f32[32,16,512]{2,1,0:T(8,128)} collective-permute-done((f32[32,16,512]{2,1,0:T(8,128)}, f32[32,16,512]{2,1,0:T(8,128)}, u32[]{:S(2)}, u32[]{:S(2)}) %collective-permute-start.1) | collective-permute-done | bytes 1048608 | tf_op jit(solution)/shard_map/ppermute | solution.py:10
  328.3 0.0 copy-done.1
  328.3 2.4 fusion.10
Async XLA Ops:
  7.2 117.1 %all-gather.5.cloned.1.call-start = ((), (), s32[]{:S(2)}) async-start(), calls=%async_computation | async-start | bytes 17825792 | tf_op jit(solution)/shard_map/all_gather | solution.py:59
  7.9 229.3 %all-gather.7.cloned.1.call-start = ((), (), s32[]{:S(2)}) async-start(), calls=%async_computation.1 | async-start | bytes 17825792 | tf_op jit(solution)/shard_map/all_gather | solution.py:64
  19.3 3.1 copy-start.3
  197.9 116.4 %collective-permute-start = (f32[32,16,512]{2,1,0:T(8,128)S(1)}, f32[32,16,512]{2,1,0:T(8,128)}, u32[]{:S(2)}, u32[]{:S(2)}) collective-permute-start(f32[32,16,512]{2,1,0:T(8,128)S(1)} %fusion.16), channel_id=1, source_target_pairs={{0,16},{16,32},{32,48},{48,64},{64,80},{80,96},{96,112},{1,17},{17... | collective-permute-start | bytes 3145736 | tf_op jit(solution)/shard_map/ppermute | solution.py:10
  265.7 3.5 %copy-start.2 = (f32[1,16,16,4,4]{2,4,3,1,0:T(4,128)S(1)}, f32[1,16,16,4,4]{2,4,3,1,0:T(4,128)}, u32[]{:S(2)}) copy-start(f32[1,16,16,4,4]{2,4,3,1,0:T(4,128)} %param.11) | copy-start | bytes 49156
  301.2 13.1 %copy-start = (f32[1,32,16,512]{3,2,1,0:T(8,128)S(1)}, f32[1,32,16,512]{3,2,1,0:T(8,128)}, u32[]{:S(2)}) copy-start(f32[1,32,16,512]{3,2,1,0:T(8,128)} %param.6) | copy-start | bytes 3145732
  301.2 27.1 %copy-start.1 = (f32[1,32,16,512]{3,2,1,0:T(8,128)S(1)}, f32[1,32,16,512]{3,2,1,0:T(8,128)}, u32[]{:S(2)}) copy-start(f32[1,32,16,512]{3,2,1,0:T(8,128)} %param.7) | copy-start | bytes 3145732
  311.6 16.7 %collective-permute-start.1 = (f32[32,16,512]{2,1,0:T(8,128)}, f32[32,16,512]{2,1,0:T(8,128)}, u32[]{:S(2)}, u32[]{:S(2)}) collective-permute-start(f32[32,16,512]{2,1,0:T(8,128)} %fusion.18), channel_id=1, source_target_pairs={{16,0},{32,16},{48,32},{64,48},{80,64},{96,80},{112,96},{17,1},{33... | collective-permute-start | bytes 3145736 | tf_op jit(solution)/shard_map/ppermute | solution.py:10
Sparse Core Ops, SparseCore 0:
  10.1 114.0 all-gather.4
  126.4 110.7 all-gather.6
where the time goes:
time: 344 us; the launch traced here: 338 us
  waiting for transfers between devices  150 us (44%)
  local copies, waits for them, and re-layouts  113 us (33%)
  matrix products  48.8 us (14%)
  between operations  14.6 us (4%)
  starting transfers between devices  6.75 us (2%)
  other arithmetic  4.81 us (1%)
    all_gather x1, waiting for transfers between devices, local(): lax.all_gather(left_environ, 'bond', axis=0, tiled=True)  101 us
    unnamed x14, local copies, waits for them, and re-layouts  46.5 us
    all_gather x1, waiting for transfers between devices, local(): lax.all_gather(right_environ, 'bond', axis=0, tiled=True)  35.3 us
    transpose x2, local copies, waits for them, and re-layouts, finish_env(): jnp.einsum('wcsb,wvst->bvct', shaped, operator, precision=lax.Precision.H...  29.1 us
    dot_general x2, local copies, waits for them, and re-layouts, finish_env(): jnp.dot(second_part.reshape(rows_dev * width, depth * states), tensor.res...  24.2 us
    dot_general x2, matrix products, finish_env(): jnp.dot(second_part.reshape(rows_dev * width, depth * states), tensor.res...  19.7 us
    dot_general x2, matrix products, add_piece(): lax.dot_general(piece.reshape(count, width * depth), columns, (((0,), (0,...  18.3 us
    ppermute x2, waiting for transfers between devices, passed_along(): return lax.ppermute(block, axis, route)  11.5 us
  transfers between devices with their start and end apart: 4, of which 3 were waited for; matrix products, arithmetic and copies ran while one was open for 49% of the time, Pallas kernels for 0%

commit v1 on v0

v1 whole, which is shorter than its diff:
```python
import jax
import jax.numpy as jnp
from jax import lax
from jax.experimental import pallas as pl
from jax.experimental.pallas import tpu as pltpu
from jax.sharding import PartitionSpec as P

MESH = pl.DeviceIdType.MESH
F32 = jnp.float32
BF16 = jnp.bfloat16


def split(value):
    high = value.astype(BF16)
    return high, (value - high.astype(F32)).astype(BF16)


def dot3(ah, al, bh, bl):
    out = jnp.dot(ah, bh, preferred_element_type=F32)
    out += jnp.dot(ah, bl, preferred_element_type=F32)
    out += jnp.dot(al, bh, preferred_element_type=F32)
    return out


def kernel(
    le, re, ls, rs, mm, nl, nr,
    buf, a1f, a2f, bdf, a1h, a1l, a2h, a2l, bdh, bdl, qh, ql, part, rcv,
    rsem, xsem, ysem, ssem, a1sem, a2sem, bdsem, a1snd, a2snd, bdsnd,
    prcv, psnd, orcv, osnd,
):
    site = lax.axis_index("site")
    bond = lax.axis_index("bond")
    z, core = site // 2, site % 2
    y, x = bond // 4, bond % 4
    sib = 1 - core
    side = x // 2
    owner = core == x % 2
    e_half = 256 * (y % 2)

    def dev(zz, cc, yy, xx):
        return (2 * zz + cc, 4 * yy + xx)

    up, down, far = (y + 1) % 4, (y + 3) % 4, (y + 2) % 4

    barrier = pltpu.get_barrier_semaphore()

    def greet(n, c):
        zz = (z + n // 8) % 4
        cc, xx = (core + (n % 8) // 4) % 2, (x + n % 4) % 4
        pl.semaphore_signal(barrier, inc=1, device_id=dev(zz, cc, y, xx), device_id_type=MESH)
        return c

    lax.fori_loop(1, 16, greet, 0)
    lax.fori_loop(24, 32, greet, 0)
    for yy in (up, down, far):
        pl.semaphore_signal(barrier, inc=1, device_id=dev(z, core, yy, x), device_id_type=MESH)
    pl.semaphore_wait(barrier, 26)

    def x_copy(sd, h):
        env = (le, re)[sd]
        return pltpu.make_async_remote_copy(
            src_ref=env.at[0, pl.ds(16 * h, 16)],
            dst_ref=buf.at[4 * h + x],
            send_sem=xsem.at[2 * sd + h],
            recv_sem=rsem.at[4 * h + x],
            device_id=dev(z, h, y, 2 * sd + core),
            device_id_type=MESH,
        )

    def is_local(sd, h):
        return (2 * sd + core == x) & (core == h)

    for sd in (0, 1):
        for h in (0, 1):
            env = (le, re)[sd]

            @pl.when(is_local(sd, h))
            def _():
                pltpu.make_async_copy(
                    env.at[0, pl.ds(16 * h, 16)], buf.at[4 * h + x], rsem.at[4 * h + x]
                ).start()

            @pl.when(jnp.logical_not(is_local(sd, h)))
            def _():
                x_copy(sd, h).start()

    def row_of(slot):
        grp, xx = slot // 4, slot % 4
        yy = (y + grp // 2 + 2 * (grp // 3)) % 4
        return 128 * yy + 32 * xx + 16 * (grp % 2)

    def a1_src(t_site, t, c):
        return t_site.at[0, :, t, pl.ds(pl.multiple_of(e_half + 128 * c, 128), 128)]

    def a1_copy(t_site, t):
        return pltpu.make_async_remote_copy(
            src_ref=a1_src(t_site, t, sib), dst_ref=a1f.at[t],
            send_sem=a1snd.at[t], recv_sem=a1sem.at[t],
            device_id=dev(z, sib, y, x), device_id_type=MESH,
        )

    def a2_copy(t_site, slot):
        return pltpu.make_async_remote_copy(
            src_ref=t_site.at[0, pl.ds(row_of(slot), 16)], dst_ref=a2f.at[slot],
            send_sem=a2snd.at[slot], recv_sem=a2sem.at[slot],
            device_id=dev(z, sib, y, x), device_id_type=MESH,
        )

    def bd_copy(sd):
        return pltpu.make_async_remote_copy(
            src_ref=mm.at[sd], dst_ref=bdf, send_sem=bdsnd, recv_sem=bdsem,
            device_id=dev(z, sib, y, x), device_id_type=MESH,
        )

    for sd in (0, 1):
        t_site = (ls, rs)[sd]

        @pl.when(owner & (side == sd))
        def _():
            for t in range(4):
                pltpu.make_async_copy(a1_src(t_site, t, core), a1f.at[t], a1sem.at[t]).start()
                a1_copy(t_site, t).start()
            pltpu.make_async_copy(mm.at[sd], bdf, bdsem).start()
            bd_copy(sd).start()

            def rows(slot, c):
                pltpu.make_async_copy(
                    t_site.at[0, pl.ds(row_of(slot), 16)], a2f.at[slot], a2sem.at[slot]
                ).start()
                a2_copy(t_site, slot).start()
                return c

            lax.fori_loop(0, 16, rows, 0)

    def block_wait(slot):
        pltpu.make_async_copy(buf.at[slot], buf.at[slot], rsem.at[slot]).wait()

    def to_sib(slot, n):
        return pltpu.make_async_remote_copy(
            src_ref=buf.at[slot], dst_ref=buf.at[slot],
            send_sem=ssem.at[n], recv_sem=rsem.at[slot],
            device_id=dev(z, sib, y, x), device_id_type=MESH,
        )

    def to_row(xx, n):
        return pltpu.make_async_remote_copy(
            src_ref=buf.at[4 * core + xx], dst_ref=buf.at[8 + 4 * core + xx],
            send_sem=ysem.at[n], recv_sem=rsem.at[8 + 4 * core + xx],
            device_id=dev(z, core, (y + 3 + 2 * core) % 4, x), device_id_type=MESH,
        )

    def col_of(i):
        return (x + i + i // 2 - 2 * (i // 3)) % 4

    for t in range(4):
        pltpu.make_async_copy(a1f.at[t], a1f.at[t], a1sem.at[t]).wait()
        a1h[:, 128 * t : 128 * (t + 1)], a1l[:, 128 * t : 128 * (t + 1)] = split(a1f[t])
    pltpu.make_async_copy(bdf, bdf, bdsem).wait()
    bdh[...], bdl[...] = split(bdf[...])

    def turn(n, c):
        for k in (0, 1):
            pltpu.make_async_copy(
                a2f.at[2 * n + k], a2f.at[2 * n + k], a2sem.at[2 * n + k]
            ).wait()
        rows = jnp.concatenate([a2f[2 * n].reshape(64, 512), a2f[2 * n + 1].reshape(64, 512)], axis=0)
        high, low = split(jnp.transpose(rows))
        a2h[:, pl.ds(pl.multiple_of(128 * n, 128), 128)] = high
        a2l[:, pl.ds(pl.multiple_of(128 * n, 128), 128)] = low
        return c

    def first_two(slot):
        lh, ll = split(buf[slot].reshape(256, 512))
        ph, pw = split(dot3(lh, ll, a1h[...], a1l[...]))

        def stack(p):
            return jnp.concatenate(
                [
                    jnp.concatenate(
                        [
                            p[64 * g + 16 * j : 64 * g + 16 * j + 16, 128 * t : 128 * t + 128]
                            for j in range(4)
                            for t in range(4)
                        ],
                        axis=0,
                    )
                    for g in range(4)
                ],
                axis=1,
            )

        oh, ol = split(dot3(bdh[...], bdl[...], stack(ph), stack(pw)))
        for g in range(4):
            at = pl.ds(pl.multiple_of(64 * slot + 16 * g, 16), 16)
            for v in range(16):
                rows, cols = slice(16 * v, 16 * v + 16), slice(128 * g, 128 * g + 128)
                qh[at, 128 * v : 128 * v + 128] = oh[rows, cols]
                ql[at, 128 * v : 128 * v + 128] = ol[rows, cols]

    def step(n, c):
        kind = n % 4
        i = n // 4 - (kind + 1) // 2

        @pl.when((i >= 0) & (i < 4))
        def _():
            xx = col_of(i)
            from_sib = kind // 2
            grp = (1 - from_sib) * (core + 2 * kind) + from_sib * (sib + 2 * (kind - 2))
            slot = 4 * grp + xx
            block_wait(slot)

            @pl.when(kind == 0)
            def _():
                to_row(xx, i).start()

            @pl.when(kind < 2)
            def _():
                to_sib(slot, 4 * kind + i).start()

            first_two(slot)

        @pl.when(n == 0)
        def _():
            lax.fori_loop(0, 8, turn, 0)

        return c

    lax.fori_loop(0, 24, step, 0)

    def last(n, row):
        lhs = pl.ds(pl.multiple_of(128 * row, 128), 128)
        flat = part.reshape(4, 2048, 128)

        def cols(i, c):
            at = pl.ds(pl.multiple_of(256 * i, 256), 256)
            out = dot3(a2h[lhs, :], a2l[lhs, :], qh[:, at], ql[:, at])
            for k in (0, 1):
                flat[n, pl.ds(2 * i + k, 128, stride=16), :] = out[:, 128 * k : 128 * k + 128]
            return c

        lax.fori_loop(0, 8, cols, 0)

    def part_copy(n, row):
        return pltpu.make_async_remote_copy(
            src_ref=part.at[n], dst_ref=rcv.at[n],
            send_sem=psnd.at[n], recv_sem=prcv.at[n],
            device_id=dev(z, core, row, x), device_id_type=MESH,
        )

    targets = (far, up, down)
    for n, row in enumerate(targets):
        last(n, row)
        part_copy(n, row).start()
    last(3, y)

    segment = 2 * z + x % 2
    target = segment + 1 - 2 * side
    valid = (target >= 0) & (target < 8)

    def out_copy(sd, n, xx):
        src = (part.at[3], rcv.at[1])[n]
        half = (y % 2) if n == 0 else 1 - y % 2
        lanes = pl.ds(pl.multiple_of(256 * half + 128 * core, 128), 128)
        out = (nl, nr)[sd]
        return pltpu.make_async_remote_copy(
            src_ref=src.at[pl.ds(32 * xx, 32)], dst_ref=out.at[0, :, :, lanes],
            send_sem=osnd.at[4 * n + xx], recv_sem=orcv.at[4 * sd + 2 * n + core],
            device_id=(target, 4 * y + xx), device_id_type=MESH,
        )

    def out_local(sd, n):
        src = (part.at[3], rcv.at[1])[n]
        half = (y % 2) if n == 0 else 1 - y % 2
        lanes = pl.ds(pl.multiple_of(256 * half + 128 * core, 128), 128)
        out = (nl, nr)[sd]
        return pltpu.make_async_copy(
            src.at[pl.ds(32 * x, 32)], out.at[0, :, :, lanes], orcv.at[4 * sd + 2 * n + core]
        )

    def hand_off(n, wait):
        for sd in (0, 1):

            @pl.when(valid & (side == sd))
            def _():
                def one(d, c):
                    xx = (x + d) % 4
                    local = (d == 0) & (target == site)

                    @pl.when(jnp.logical_not(local))
                    def _():
                        if wait:
                            out_copy(sd, n, xx).wait_send()
                        else:
                            out_copy(sd, n, xx).start()

                    if not wait:

                        @pl.when(local)
                        def _():
                            out_local(sd, n).start()

                    return c

                lax.fori_loop(0, 4, one, 0)

    part_copy(1, up).wait_recv()
    part_copy(2, down).wait_recv()

    def add_one(i, c):
        at = pl.ds(8 * i, 8)
        rcv[1, at] = rcv[1, at] + rcv[2, at]
        return c

    lax.fori_loop(0, 16, add_one, 0)
    hand_off(1, False)
    part_copy(0, far).wait_recv()

    def add_zero(i, c):
        at = pl.ds(8 * i, 8)
        part[3, at] = part[3, at] + rcv[0, at]
        return c

    lax.fori_loop(0, 16, add_zero, 0)
    hand_off(0, False)

    for sd in (0, 1):
        for h in (0, 1):

            @pl.when(jnp.logical_not(is_local(sd, h)))
            def _():
                x_copy(sd, h).wait_send()

    for i in range(4):
        to_row(col_of(i), i).wait_send()
        to_sib(4 * core + col_of(i), i).wait_send()
        to_sib(8 + 4 * core + col_of(i), 4 + i).wait_send()
    for sd in (0, 1):
        t_site = (ls, rs)[sd]

        @pl.when(owner & (side == sd))
        def _():
            for t in range(4):
                a1_copy(t_site, t).wait_send()
            bd_copy(sd).wait_send()

            def rows(slot, c):
                a2_copy(t_site, slot).wait_send()
                return c

            lax.fori_loop(0, 16, rows, 0)

    for n, row in enumerate(targets):
        part_copy(n, row).wait_send()
    hand_off(1, True)
    hand_off(0, True)
    for sd in (0, 1):

        @pl.when((site > 0) if sd == 0 else (site < 7))
        def _():
            out = (nl, nr)[sd]
            for k in range(4):
                block = out.at[0, :, :, pl.ds(128 * k, 128)]
                pltpu.make_async_copy(block, block, orcv.at[4 * sd + k]).wait()


def grow(left_env, right_env, left_site, right_site, operators):
    any_space = pl.BlockSpec(memory_space=pl.ANY)
    dma = pltpu.SemaphoreType.DMA
    vmem = pltpu.VMEM
    return pl.pallas_call(
        kernel,
        out_shape=[jax.ShapeDtypeStruct(left_env.shape, F32)] * 2,
        in_specs=[any_space] * 5,
        out_specs=[any_space] * 2,
        scratch_shapes=[
            vmem((16, 16, 16, 512), F32),
            vmem((4, 512, 128), F32),
            vmem((16, 16, 4, 512), F32),
            vmem((256, 256), F32),
            vmem((512, 512), BF16),
            vmem((512, 512), BF16),
            vmem((512, 1024), BF16),
            vmem((512, 1024), BF16),
            vmem((256, 256), BF16),
            vmem((256, 256), BF16),
            vmem((1024, 2048), BF16),
            vmem((1024, 2048), BF16),
            vmem((4, 128, 16, 128), F32),
            vmem((3, 128, 16, 128), F32),
            dma((16,)), dma((4,)), dma((4,)), dma((8,)),
            dma((4,)), dma((16,)), dma, dma((4,)), dma((16,)), dma,
            dma((3,)), dma((3,)), dma((8,)), dma((8,)),
        ],
        compiler_params=pltpu.CompilerParams(
            collective_id=0, has_side_effects=True, vmem_limit_bytes=62 * 1024 * 1024
        ),
    )(left_env, right_env, left_site, right_site, operators)


def spread(operator):
    states = operator.shape[2]
    width = operator.shape[0]
    same = jnp.eye(states, dtype=jnp.bool_)[None, :, None, :, None, None]
    whole = jnp.where(same, operator.transpose(1, 2, 3, 0)[:, None, :, None], 0.0)
    return whole.reshape(width * states * states, width * states * states)


def local(left_env, right_env, left_site, right_site, left_mpo, right_mpo):
    operators = jnp.stack(
        [spread(left_mpo[0]), spread(jnp.transpose(right_mpo[0], (1, 0, 2, 3)))]
    )
    from_left, from_right = grow(left_env, right_env, left_site, right_site, operators)
    segment = lax.axis_index("site")
    last_segment = lax.axis_size("site") - 1
    new_left = jnp.where(segment == 0, left_env, from_left)
    new_right = jnp.where(segment == last_segment, right_env, from_right)
    return (new_left, new_right)


def solution(mesh):
    return jax.shard_map(
        local,
        mesh=mesh,
        in_specs=(
            P("site", "bond", None, None),
            P("site", "bond", None, None),
            P("site", None, None, None),
            P("site", None, None, None),
            P("site", None, None, None, None),
            P("site", None, None, None, None),
        ),
        out_specs=(P("site", "bond", None, None), P("site", "bond", None, None)),
        check_vma=False,
    )
```

time: 344 us -> 146 us (0.42)
  the two profiles are of different devices: /device:TPU:1 before, /device:TPU:5 now
where the time goes in v1:
time: 146 us; the launch traced here: 144 us
  Pallas kernels  129 us (88%)
  other arithmetic  7.79 us (5%)
  local copies, waits for them, and re-layouts  6.44 us (4%)
    pallas_call x1, Pallas kernels, grow(): pl.pallas_call(kernel, out_shape=[jax.ShapeDtypeStruct(left_env.shape, F3...  129 us
    select_n x2, local copies, waits for them, and re-layouts, spread(): jnp.where(same, operator.transpose(1, 2, 3, 0)[:, None, :, None], 0.0)  5.4 us
    select_n x1, other arithmetic, local(): new_right = jnp.where(segment == last_segment, right_env, from_right)  3.55 us
    select_n x1, other arithmetic, spread(): jnp.where(same, operator.transpose(1, 2, 3, 0)[:, None, :, None], 0.0)  3.41 us

profile of v1, /device:TPU:5, one launch (start us, length us, event | category | flops | bytes accessed | tf_op | source)
XLA Modules:
  0.0 144.3 jit_solution(4399322503733839007)
XLA Ops:
  0.6 1.0 copy.8
  1.7 3.4 %broadcast_select_fusion.1 = (f32[16,4,4,4,4,16]{5,4,3,2,1,0:T(4,128)}, f32[16,4,4,4,4,16]{5,4,3,2,1,0:T(4,128)S(1)}) fusion(f32[16,4,4,16]{3,2,1,0:T(4,128)S(1)} %copy.8, pred[4,4]{1,0:T(4,128)(4,1)S(1)} %iota_compare_fusion, f32[16,4,4,16]{3,2,1,0:T(4,128)} %bitcast.6), kind=kLoop, calls=%fused_computation.1 | loop fusion | flops 131072 | bytes 557072 | tf_op jit(solution)/shard_map/jit(_where)/select_n | solution.py:404
  5.1 3.4 %select_n.43 = f32[1,256,256]{2,1,0:T(8,128)S(1)} reshape(f32[16,4,4,4,4,16]{5,4,3,2,1,0:T(4,128)} %get-tuple-element.6) | data formatting | bytes 524288 | tf_op jit(solution)/shard_map/jit(_where)/select_n | solution.py:404
  8.5 2.0 %select_n.45 = f32[1,256,256]{2,1,0:T(8,128)S(1)} reshape(f32[16,4,4,4,4,16]{5,4,3,2,1,0:T(4,128)S(1)} %get-tuple-element.7) | data formatting | bytes 524288 | tf_op jit(solution)/shard_map/jit(_where)/select_n | solution.py:404
  10.5 0.8 pad_maximum_fusion.mm
  11.3 0.0 copy-start
  11.3 129.4 %shard_map.77 = (f32[1,32,16,512]{3,2,1,0:T(8,128)}, f32[1,32,16,512]{3,2,1,0:T(8,128)}) custom-call(f32[1,32,16,512]{3,2,1,0:T(8,128)} %le.1, f32[1,32,16,512]{3,2,1,0:T(8,128)} %re.1, f32[1,512,4,512]{3,2,1,0:T(4,128)} %ls.1, f32[1,512,4,512]{3,2,1,0:T(4,128)} %rs.1, f32[2,256,256]{2,1,0:T(8,128)} %pad_maximum_fusion.mm), custom_call_target="tpu_custom_call" | custom-call | tf_op jit(solution)/shard_map/pallas_call | solution.py:370
  140.8 0.0 copy-done
  140.8 3.5 %broadcast_select_fusion.2 = (f32[1,32,16,512]{3,2,1,0:T(8,128)}, f32[1,32,16,512]{3,2,1,0:T(8,128)}) fusion(f32[1,32,16,512]{3,2,1,0:T(8,128)S(1)} %copy-done, f32[1,32,16,512]{3,2,1,0:T(8,128)} %get-tuple-element.5, pred[]{:T(512)S(6)} %eq.18, f32[1,32,16,512]{3,2,1,0:T(8,128)} %le.1, f32[1,32,16,512]{3,2,1,0:T(8,128)} %get-tuple-element.4, pred[]{:T(512)S(6)} %eq.16), kind=kLoop, calls=%fused_computation.3 | loop fusion | flops 524288 | bytes 6291458 | tf_op jit(solution)/shard_map/jit(_where)/select_n | solution.py:416
  (1 shorter events, 0.0 us)
Async XLA Ops:
  11.3 129.4 %copy-start = (f32[1,32,16,512]{3,2,1,0:T(8,128)S(1)}, f32[1,32,16,512]{3,2,1,0:T(8,128)}, u32[]{:S(2)}) copy-start(f32[1,32,16,512]{3,2,1,0:T(8,128)} %re.1) | copy-start | bytes 3145732

commit v2 on v1

--- a/solution.py
+++ b/solution.py
@@ -8,6 +8,7 @@
 MESH = pl.DeviceIdType.MESH
 F32 = jnp.float32
 BF16 = jnp.bfloat16
+DELAY = 1
 
 
 def split(value):
@@ -23,10 +24,10 @@
 
 
 def kernel(
-    le, re, ls, rs, mm, nl, nr,
-    buf, a1f, a2f, bdf, a1h, a1l, a2h, a2l, bdh, bdl, qh, ql, part, rcv,
-    rsem, xsem, ysem, ssem, a1sem, a2sem, bdsem, a1snd, a2snd, bdsnd,
-    prcv, psnd, orcv, osnd,
+    le, re, ls, rs, lm, rm, nl, nr,
+    buf, a1f, a2f, mpo, a1h, a1l, a2h, a2l, bdh, bdl, qh, ql, part, rcv, kept,
+    rsem, xrcv, xsem, ysem, ssem, a1sem, a2sem, mposem, a1snd, a2snd, mposnd,
+    prcv, psnd, orcv, osnd, ksem,
 ):
     site = lax.axis_index("site")
     bond = lax.axis_index("bond")
@@ -56,33 +57,51 @@
         pl.semaphore_signal(barrier, inc=1, device_id=dev(z, core, yy, x), device_id_type=MESH)
     pl.semaphore_wait(barrier, 26)
 
-    def x_copy(sd, h):
+    def x_copy(sd, h, lo, count, sem):
         env = (le, re)[sd]
         return pltpu.make_async_remote_copy(
-            src_ref=env.at[0, pl.ds(16 * h, 16)],
-            dst_ref=buf.at[4 * h + x],
+            src_ref=env.at[0, pl.ds(16 * h + lo, count)],
+            dst_ref=buf.at[4 * h + x, pl.ds(lo, count)],
             send_sem=xsem.at[2 * sd + h],
-            recv_sem=rsem.at[4 * h + x],
+            recv_sem=xrcv.at[x, sem],
             device_id=dev(z, h, y, 2 * sd + core),
             device_id_type=MESH,
         )
 
-    def is_local(sd, h):
-        return (2 * sd + core == x) & (core == h)
-
-    for sd in (0, 1):
-        for h in (0, 1):
-            env = (le, re)[sd]
-
-            @pl.when(is_local(sd, h))
-            def _():
-                pltpu.make_async_copy(
-                    env.at[0, pl.ds(16 * h, 16)], buf.at[4 * h + x], rsem.at[4 * h + x]
-                ).start()
-
-            @pl.when(jnp.logical_not(is_local(sd, h)))
-            def _():
-                x_copy(sd, h).start()
+    def hops(sd):
+        return (2 * sd + core + 4 - x) % 4
+
+    def pieces(sd):
+        for k in range(4):
+            for h in (0, 1):
+                x_copy(sd, h, 4 * k, 4, k).start()
+
+    for sd in (0, 1):
+
+        @pl.when(hops(sd) % 2 == 1)
+        def _():
+            pieces(sd)
+
+        @pl.when(hops(sd) == 0)
+        def _():
+            for h in (0, 1):
+
+                @pl.when(core == h)
+                def _():
+                    pltpu.make_async_copy(
+                        (le, re)[sd].at[0, pl.ds(16 * h, 16)], buf.at[4 * h + x], xrcv.at[x, 0]
+                    ).start()
+
+                @pl.when(core != h)
+                def _():
+                    x_copy(sd, h, 0, 16, 0).start()
+
+    keeps = (site == 0, site == 7)
+    for sd in (0, 1):
+
+        @pl.when(keeps[sd])
+        def _():
+            pltpu.make_async_copy((le, re)[sd].at[0], kept, ksem).start()
 
     def row_of(slot):
         grp, xx = slot // 4, slot % 4
@@ -106,9 +125,9 @@
             device_id=dev(z, sib, y, x), device_id_type=MESH,
         )
 
-    def bd_copy(sd):
-        return pltpu.make_async_remote_copy(
-            src_ref=mm.at[sd], dst_ref=bdf, send_sem=bdsnd, recv_sem=bdsem,
+    def mpo_copy(sd):
+        return pltpu.make_async_remote_copy(
+            src_ref=(lm, rm)[sd], dst_ref=mpo, send_sem=mposnd, recv_sem=mposem,
             device_id=dev(z, sib, y, x), device_id_type=MESH,
         )
 
@@ -120,8 +139,8 @@
             for t in range(4):
                 pltpu.make_async_copy(a1_src(t_site, t, core), a1f.at[t], a1sem.at[t]).start()
                 a1_copy(t_site, t).start()
-            pltpu.make_async_copy(mm.at[sd], bdf, bdsem).start()
-            bd_copy(sd).start()
+            pltpu.make_async_copy((lm, rm)[sd], mpo, mposem).start()
+            mpo_copy(sd).start()
 
             def rows(slot, c):
                 pltpu.make_async_copy(
@@ -142,21 +161,59 @@
             device_id=dev(z, sib, y, x), device_id_type=MESH,
         )
 
-    def to_row(xx, n):
-        return pltpu.make_async_remote_copy(
-            src_ref=buf.at[4 * core + xx], dst_ref=buf.at[8 + 4 * core + xx],
-            send_sem=ysem.at[n], recv_sem=rsem.at[8 + 4 * core + xx],
+    def to_row(xx, lo, count):
+        return pltpu.make_async_remote_copy(
+            src_ref=buf.at[4 * core + xx, pl.ds(lo, count)],
+            dst_ref=buf.at[8 + 4 * core + xx, pl.ds(lo, count)],
+            send_sem=ysem.at[xx], recv_sem=rsem.at[8 + 4 * core + xx],
             device_id=dev(z, core, (y + 3 + 2 * core) % 4, x), device_id_type=MESH,
         )
+
+    def x_wait(xx, lo, count, sem):
+        at = buf.at[4 * core + xx, pl.ds(lo, count)]
+        pltpu.make_async_copy(at, at, xrcv.at[xx, sem]).wait()
 
     def col_of(i):
         return (x + i + i // 2 - 2 * (i // 3)) % 4
+
+    x_wait(x, 0, 16, 0)
+    to_row(x, 0, 16).start()
+    to_sib(4 * core + x, 0).start()
+
+    pltpu.make_async_copy(mpo, mpo, mposem).wait()
+    small = split(mpo[...].reshape(256, 16))
+    row = lax.broadcasted_iota(jnp.int32, (256, 256), 0)
+    col = lax.broadcasted_iota(jnp.int32, (256, 256), 1)
+    diagonal = ((row >> 2) & 3) == (col >> 6)
+
+    def ones(mask):
+        return jnp.where(mask, 1.0, 0.0).astype(BF16)
+
+    @pl.when(side == 0)
+    def _():
+        pick = ones((lax.broadcasted_iota(jnp.int32, (256, 16), 0) >> 4)
+                    == lax.broadcasted_iota(jnp.int32, (256, 16), 1))
+        move = ones(((row >> 4) == (col & 15)) & ((row & 3) == ((col >> 4) & 3)))
+        for value, ref in zip(small, (bdh, bdl)):
+            wide = lax.dot_general(pick, value, (((1,), (1,)), ((), ())), preferred_element_type=F32)
+            wide = jnp.where(((col >> 2) & 3) == (row & 3), wide, 0.0).astype(BF16)
+            out = jnp.dot(wide, move, preferred_element_type=F32)
+            ref[...] = jnp.where(diagonal, out, 0.0).astype(BF16)
+
+    @pl.when(side == 1)
+    def _():
+        pick = ones((lax.broadcasted_iota(jnp.int32, (16, 256), 1) & 15)
+                    == lax.broadcasted_iota(jnp.int32, (16, 256), 0))
+        move = ones(((col >> 4) == (row >> 4)) & (((col >> 2) & 3) == (row & 3)))
+        for value, ref in zip(small, (bdh, bdl)):
+            wide = jnp.dot(value, pick, preferred_element_type=F32)
+            wide = jnp.where((row & 3) == ((col >> 4) & 3), wide, 0.0).astype(BF16)
+            out = jnp.dot(move, wide, preferred_element_type=F32)
+            ref[...] = jnp.where(diagonal, out, 0.0).astype(BF16)
 
     for t in range(4):
         pltpu.make_async_copy(a1f.at[t], a1f.at[t], a1sem.at[t]).wait()
         a1h[:, 128 * t : 128 * (t + 1)], a1l[:, 128 * t : 128 * (t + 1)] = split(a1f[t])
-    pltpu.make_async_copy(bdf, bdf, bdsem).wait()
-    bdh[...], bdl[...] = split(bdf[...])
 
     def turn(n, c):
         for k in (0, 1):
@@ -207,13 +264,27 @@
             from_sib = kind // 2
             grp = (1 - from_sib) * (core + 2 * kind) + from_sib * (sib + 2 * (kind - 2))
             slot = 4 * grp + xx
-            block_wait(slot)
-
-            @pl.when(kind == 0)
+
+            @pl.when((kind == 0) & (i > 0))
             def _():
-                to_row(xx, i).start()
-
-            @pl.when(kind < 2)
+                for k in range(4):
+                    x_wait(xx, 4 * k, 4, k)
+                    to_row(xx, 4 * k, 4).start()
+                    if k == DELAY:
+
+                        @pl.when(i == 1)
+                        def _():
+                            for sd in (0, 1):
+
+                                @pl.when(hops(sd) == 2)
+                                def _():
+                                    pieces(sd)
+
+            @pl.when(kind > 0)
+            def _():
+                block_wait(slot)
+
+            @pl.when((kind == 1) | ((kind == 0) & (i > 0)))
             def _():
                 to_sib(slot, 4 * kind + i).start()
 
@@ -240,17 +311,22 @@
 
         lax.fori_loop(0, 8, cols, 0)
 
-    def part_copy(n, row):
-        return pltpu.make_async_remote_copy(
-            src_ref=part.at[n], dst_ref=rcv.at[n],
-            send_sem=psnd.at[n], recv_sem=prcv.at[n],
+    def part_copy(n, row, i):
+        at = pl.ds(32 * end_of(i), 32)
+        return pltpu.make_async_remote_copy(
+            src_ref=part.at[n, at], dst_ref=rcv.at[n, at],
+            send_sem=psnd.at[n, i], recv_sem=prcv.at[n, i],
             device_id=dev(z, core, row, x), device_id_type=MESH,
         )
+
+    def end_of(i):
+        return (x + 2 + i + i // 2 - 2 * (i // 3)) % 4
 
     targets = (far, up, down)
     for n, row in enumerate(targets):
         last(n, row)
-        part_copy(n, row).start()
+        for i in range(4):
+            part_copy(n, row, i).start()
     last(3, y)
 
     segment = 2 * z + x % 2
@@ -277,61 +353,61 @@
             src.at[pl.ds(32 * x, 32)], out.at[0, :, :, lanes], orcv.at[4 * sd + 2 * n + core]
         )
 
-    def hand_off(n, wait):
+    def hand_off(n, xx, wait):
+        local = (xx == x) & (target == site)
         for sd in (0, 1):
 
             @pl.when(valid & (side == sd))
             def _():
-                def one(d, c):
-                    xx = (x + d) % 4
-                    local = (d == 0) & (target == site)
-
-                    @pl.when(jnp.logical_not(local))
+                @pl.when(jnp.logical_not(local))
+                def _():
+                    if wait:
+                        out_copy(sd, n, xx).wait_send()
+                    else:
+                        out_copy(sd, n, xx).start()
+
+                if not wait:
+
+                    @pl.when(local)
                     def _():
-                        if wait:
-                            out_copy(sd, n, xx).wait_send()
-                        else:
-                            out_copy(sd, n, xx).start()
-
-                    if not wait:
-
-                        @pl.when(local)
-                        def _():
-                            out_local(sd, n).start()
-
-                    return c
-
-                lax.fori_loop(0, 4, one, 0)
-
-    part_copy(1, up).wait_recv()
-    part_copy(2, down).wait_recv()
-
-    def add_one(i, c):
-        at = pl.ds(8 * i, 8)
-        rcv[1, at] = rcv[1, at] + rcv[2, at]
-        return c
-
-    lax.fori_loop(0, 16, add_one, 0)
-    hand_off(1, False)
-    part_copy(0, far).wait_recv()
-
-    def add_zero(i, c):
-        at = pl.ds(8 * i, 8)
-        part[3, at] = part[3, at] + rcv[0, at]
-        return c
-
-    lax.fori_loop(0, 16, add_zero, 0)
-    hand_off(0, False)
+                        out_local(sd, n).start()
+
+    for sd in (0, 1):
+
+        @pl.when(keeps[sd])
+        def _():
+            pltpu.make_async_copy((le, re)[sd].at[0], kept, ksem).wait()
+            pltpu.make_async_copy(kept, (nl, nr)[sd].at[0], ksem).start()
+
+    def finish(n, xx):
+        def add(k, c):
+            at = pl.ds(32 * xx + 8 * k, 8)
+            if n == 0:
+                part[3, at] = part[3, at] + rcv[0, at]
+            else:
+                rcv[1, at] = rcv[1, at] + rcv[2, at]
+            return c
+
+        lax.fori_loop(0, 4, add, 0)
+        hand_off(n, xx, False)
+
+    for i in range(4):
+        part_copy(0, far, i).wait_recv()
+        finish(0, end_of(i))
+    for i in range(4):
+        part_copy(1, up, i).wait_recv()
+        part_copy(2, down, i).wait_recv()
+        finish(1, end_of(i))
 
     for sd in (0, 1):
         for h in (0, 1):
 
-            @pl.when(jnp.logical_not(is_local(sd, h)))
+            @pl.when((hops(sd) != 0) | (core != h))
             def _():
-                x_copy(sd, h).wait_send()
+                x_copy(sd, h, 0, 16, 0).wait_send()
 
     for i in range(4):
-        to_row(col_of(i), i).wait_send()
+        to_row(col_of(i), 0, 16).wait_send()
         to_sib(4 * core + col_of(i), i).wait_send()
         to_sib(8 + 4 * core + col_of(i), 4 + i).wait_send()
     for sd in (0, 1):
@@ -341,7 +417,7 @@
         def _():
             for t in range(4):
                 a1_copy(t_site, t).wait_send()
-            bd_copy(sd).wait_send()
+            mpo_copy(sd).wait_send()
 
             def rows(slot, c):
                 a2_copy(t_site, slot).wait_send()
@@ -350,9 +426,11 @@
             lax.fori_loop(0, 16, rows, 0)
 
     for n, row in enumerate(targets):
-        part_copy(n, row).wait_send()
-    hand_off(1, True)
-    hand_off(0, True)
+        for i in range(4):
+            part_copy(n, row, i).wait_send()
+    for i in range(4):
+        for n in (0, 1):
+            hand_off(n, end_of(i), True)
     for sd in (0, 1):
 
         @pl.when((site > 0) if sd == 0 else (site < 7))
@@ -362,21 +440,25 @@
                 block = out.at[0, :, :, pl.ds(128 * k, 128)]
                 pltpu.make_async_copy(block, block, orcv.at[4 * sd + k]).wait()
 
-
-def grow(left_env, right_env, left_site, right_site, operators):
+        @pl.when(keeps[sd])
+        def _():
+            pltpu.make_async_copy(kept, (nl, nr)[sd].at[0], ksem).wait()
+
+
+def grow(left_env, right_env, left_site, right_site, left_mpo, right_mpo):
     any_space = pl.BlockSpec(memory_space=pl.ANY)
     dma = pltpu.SemaphoreType.DMA
     vmem = pltpu.VMEM
     return pl.pallas_call(
         kernel,
         out_shape=[jax.ShapeDtypeStruct(left_env.shape, F32)] * 2,
-        in_specs=[any_space] * 5,
+        in_specs=[any_space] * 6,
         out_specs=[any_space] * 2,
         scratch_shapes=[
             vmem((16, 16, 16, 512), F32),
             vmem((4, 512, 128), F32),
             vmem((16, 16, 4, 512), F32),
-            vmem((256, 256), F32),
+            vmem((16, 4, 4, 16), F32),
             vmem((512, 512), BF16),
             vmem((512, 512), BF16),
             vmem((512, 1024), BF16),
@@ -387,34 +469,24 @@
             vmem((1024, 2048), BF16),
             vmem((4, 128, 16, 128), F32),
             vmem((3, 128, 16, 128), F32),
-            dma((16,)), dma((4,)), dma((4,)), dma((8,)),
+            vmem((32, 16, 512), F32),
+            dma((16,)), dma((4, 4)), dma((4,)), dma((4,)), dma((8,)),
             dma((4,)), dma((16,)), dma, dma((4,)), dma((16,)), dma,
-            dma((3,)), dma((3,)), dma((8,)), dma((8,)),
+            dma((3, 4)), dma((3, 4)), dma((8,)), dma((8,)), dma,
         ],
         compiler_params=pltpu.CompilerParams(
             collective_id=0, has_side_effects=True, vmem_limit_bytes=62 * 1024 * 1024
         ),
-    )(left_env, right_env, left_site, right_site, operators)
-
-
-def spread(operator):
-    states = operator.shape[2]
-    width = operator.shape[0]
-    same = jnp.eye(states, dtype=jnp.bool_)[None, :, None, :, None, None]
-    whole = jnp.where(same, operator.transpose(1, 2, 3, 0)[:, None, :, None], 0.0)
-    return whole.reshape(width * states * states, width * states * states)
+    )(left_env, right_env, left_site, right_site, left_mpo, right_mpo)
 
 
 def local(left_env, right_env, left_site, right_site, left_mpo, right_mpo):
-    operators = jnp.stack(
-        [spread(left_mpo[0]), spread(jnp.transpose(right_mpo[0], (1, 0, 2, 3)))]
+    def turned(operator):
+        return jnp.transpose(operator[0], (0, 2, 3, 1))
+
+    return tuple(
+        grow(left_env, right_env, left_site, right_site, turned(left_mpo), turned(right_mpo))
     )
-    from_left, from_right = grow(left_env, right_env, left_site, right_site, operators)
-    segment = lax.axis_index("site")
-    last_segment = lax.axis_size("site") - 1
-    new_left = jnp.where(segment == 0, left_env, from_left)
-    new_right = jnp.where(segment == last_segment, right_env, from_right)
-    return (new_left, new_right)
 
 
 def solution(mesh):

time: 146 us -> 109 us (0.75)
  the two profiles are of different devices: /device:TPU:5 before, /device:TPU:69 now
where the time goes in v2:
time: 109 us
  Pallas kernels  104 us (95%)
  local copies, waits for them, and re-layouts  4.61 us (4%)
    pallas_call x1, Pallas kernels, grow(): pl.pallas_call(kernel, out_shape=[jax.ShapeDtypeStruct(left_env.shape, F3...  104 us
    unnamed x2, local copies, waits for them, and re-layouts  4.61 us

profile of v2, /device:TPU:69, one launch (start us, length us, event | category | flops | bytes accessed | tf_op | source)
XLA Modules:
  0.0 109.0 jit_solution(5288818465723083967)
XLA Ops:
  0.6 103.7 %shard_map.77 = (f32[1,32,16,512]{3,2,1,0:T(8,128)}, f32[1,32,16,512]{3,2,1,0:T(8,128)}) custom-call(f32[1,32,16,512]{3,2,1,0:T(8,128)} %le.1, f32[1,32,16,512]{3,2,1,0:T(8,128)} %re.1, f32[1,512,4,512]{3,2,1,0:T(4,128)} %ls.1, f32[1,512,4,512]{3,2,1,0:T(4,128)} %rs.1, f32[16,4,4,16]{3,2,1,0:T(4,128)} %bitcast.6, f32[16,4,4,16]{3,2,1,0:T(4,128)} %bitcast.7), custom_call_target="tpu_custom_call" | custom-call | tf_op jit(solution)/shard_map/pallas_call | solution.py:452
  104.4 2.3 %copy.10 = f32[1,32,16,512]{3,2,1,0:T(8,128)} copy(f32[1,32,16,512]{3,2,1,0:T(8,128)} %get-tuple-element.4) | data formatting | bytes 2097152
  106.7 2.3 %copy.11 = f32[1,32,16,512]{3,2,1,0:T(8,128)} copy(f32[1,32,16,512]{3,2,1,0:T(8,128)} %get-tuple-element.5) | data formatting | bytes 2097152

commit v3 on v2

--- a/solution.py
+++ b/solution.py
@@ -8,7 +8,6 @@
 MESH = pl.DeviceIdType.MESH
 F32 = jnp.float32
 BF16 = jnp.bfloat16
-DELAY = 1
 
 
 def split(value):
@@ -27,7 +26,7 @@
     le, re, ls, rs, lm, rm, nl, nr,
     buf, a1f, a2f, mpo, a1h, a1l, a2h, a2l, bdh, bdl, qh, ql, part, rcv, kept,
     rsem, xrcv, xsem, ysem, ssem, a1sem, a2sem, mposem, a1snd, a2snd, mposnd,
-    prcv, psnd, orcv, osnd, ksem,
+    prcv, psnd, orcv, osnd, ksem, near,
 ):
     site = lax.axis_index("site")
     bond = lax.axis_index("bond")
@@ -46,16 +45,24 @@
     barrier = pltpu.get_barrier_semaphore()
 
     def greet(n, c):
-        zz = (z + n // 8) % 4
-        cc, xx = (core + (n % 8) // 4) % 2, (x + n % 4) % 4
-        pl.semaphore_signal(barrier, inc=1, device_id=dev(zz, cc, y, xx), device_id_type=MESH)
+        there = dev(z, (core + n // 4) % 2, y, (x + n % 4) % 4)
+        pl.semaphore_signal(barrier, inc=1, device_id=there, device_id_type=MESH)
         return c
 
-    lax.fori_loop(1, 16, greet, 0)
-    lax.fori_loop(24, 32, greet, 0)
+    lax.fori_loop(1, 8, greet, 0)
     for yy in (up, down, far):
         pl.semaphore_signal(barrier, inc=1, device_id=dev(z, core, yy, x), device_id_type=MESH)
-    pl.semaphore_wait(barrier, 26)
+    above, below = z < 3, z > 0
+    for there, step in ((above, 1), (below, -1)):
+
+        @pl.when(there)
+        def _():
+            for cc in (0, 1):
+                pl.semaphore_signal(
+                    barrier, inc=1, device_id=dev(z + step, cc, y, x), device_id_type=MESH
+                )
+
+    pl.semaphore_wait(barrier, 10 + 2 * jnp.where(above, 1, 0) + 2 * jnp.where(below, 1, 0))
 
     def x_copy(sd, h, lo, count, sem):
         env = (le, re)[sd]
@@ -96,6 +103,13 @@
                 def _():
                     x_copy(sd, h, 0, 16, 0).start()
 
+    def tell(n, c):
+        there = dev(z, (core + n // 4) % 2, y, (x + n % 4) % 4)
+        pl.semaphore_signal(near, inc=1, device_id=there, device_id_type=MESH)
+        return c
+
+    lax.fori_loop(1, 8, tell, 0)
+
     keeps = (site == 0, site == 7)
     for sd in (0, 1):
 
@@ -142,6 +156,39 @@
             pltpu.make_async_copy((lm, rm)[sd], mpo, mposem).start()
             mpo_copy(sd).start()
 
+    def block_wait(slot):
+        pltpu.make_async_copy(buf.at[slot], buf.at[slot], rsem.at[slot]).wait()
+
+    def to_sib(slot, n):
+        return pltpu.make_async_remote_copy(
+            src_ref=buf.at[slot], dst_ref=buf.at[slot],
+            send_sem=ssem.at[n], recv_sem=rsem.at[slot],
+            device_id=dev(z, sib, y, x), device_id_type=MESH,
+        )
+
+    def to_row(xx, lo, count):
+        return pltpu.make_async_remote_copy(
+            src_ref=buf.at[4 * core + xx, pl.ds(lo, count)],
+            dst_ref=buf.at[8 + 4 * core + xx, pl.ds(lo, count)],
+            send_sem=ysem.at[xx], recv_sem=rsem.at[8 + 4 * core + xx],
+            device_id=dev(z, core, (y + 3 + 2 * core) % 4, x), device_id_type=MESH,
+        )
+
+    def x_wait(xx, lo, count, sem):
+        at = buf.at[4 * core + xx, pl.ds(lo, count)]
+        pltpu.make_async_copy(at, at, xrcv.at[xx, sem]).wait()
+
+    def col_of(i):
+        return (x + i + i // 2 - 2 * (i // 3)) % 4
+
+    x_wait(x, 0, 16, 0)
+    to_row(x, 0, 16).start()
+    to_sib(4 * core + x, 0).start()
+    for sd in (0, 1):
+        t_site = (ls, rs)[sd]
+
+        @pl.when(owner & (side == sd))
+        def _():
             def rows(slot, c):
                 pltpu.make_async_copy(
                     t_site.at[0, pl.ds(row_of(slot), 16)], a2f.at[slot], a2sem.at[slot]
@@ -151,34 +198,18 @@
 
             lax.fori_loop(0, 16, rows, 0)
 
-    def block_wait(slot):
-        pltpu.make_async_copy(buf.at[slot], buf.at[slot], rsem.at[slot]).wait()
-
-    def to_sib(slot, n):
-        return pltpu.make_async_remote_copy(
-            src_ref=buf.at[slot], dst_ref=buf.at[slot],
-            send_sem=ssem.at[n], recv_sem=rsem.at[slot],
-            device_id=dev(z, sib, y, x), device_id_type=MESH,
-        )
-
-    def to_row(xx, lo, count):
-        return pltpu.make_async_remote_copy(
-            src_ref=buf.at[4 * core + xx, pl.ds(lo, count)],
-            dst_ref=buf.at[8 + 4 * core + xx, pl.ds(lo, count)],
-            send_sem=ysem.at[xx], recv_sem=rsem.at[8 + 4 * core + xx],
-            device_id=dev(z, core, (y + 3 + 2 * core) % 4, x), device_id_type=MESH,
-        )
-
-    def x_wait(xx, lo, count, sem):
-        at = buf.at[4 * core + xx, pl.ds(lo, count)]
-        pltpu.make_async_copy(at, at, xrcv.at[xx, sem]).wait()
-
-    def col_of(i):
-        return (x + i + i // 2 - 2 * (i // 3)) % 4
-
-    x_wait(x, 0, 16, 0)
-    to_row(x, 0, 16).start()
-    to_sib(4 * core + x, 0).start()
+    def pass_on(i, k):
+        x_wait(col_of(i), 4 * k, 4, k)
+        to_row(col_of(i), 4 * k, 4).start()
+
+    def start_far():
+        for sd in (0, 1):
+
+            @pl.when(hops(sd) == 2)
+            def _():
+                pieces(sd)
+
+    pass_on(1, 0)
 
     pltpu.make_async_copy(mpo, mpo, mposem).wait()
     small = split(mpo[...].reshape(256, 16))
@@ -211,9 +242,17 @@
             out = jnp.dot(move, wide, preferred_element_type=F32)
             ref[...] = jnp.where(diagonal, out, 0.0).astype(BF16)
 
+    pass_on(1, 1)
     for t in range(4):
         pltpu.make_async_copy(a1f.at[t], a1f.at[t], a1sem.at[t]).wait()
         a1h[:, 128 * t : 128 * (t + 1)], a1l[:, 128 * t : 128 * (t + 1)] = split(a1f[t])
+
+    pass_on(1, 2)
+    pass_on(1, 3)
+    start_far()
+    to_sib(4 * core + col_of(1), 1).start()
+    for k in range(4):
+        pass_on(2, k)
 
     def turn(n, c):
         for k in (0, 1):
@@ -265,26 +304,16 @@
             grp = (1 - from_sib) * (core + 2 * kind) + from_sib * (sib + 2 * (kind - 2))
             slot = 4 * grp + xx
 
-            @pl.when((kind == 0) & (i > 0))
+            @pl.when((kind == 0) & (i == 3))
             def _():
                 for k in range(4):
-                    x_wait(xx, 4 * k, 4, k)
-                    to_row(xx, 4 * k, 4).start()
-                    if k == DELAY:
-
-                        @pl.when(i == 1)
-                        def _():
-                            for sd in (0, 1):
-
-                                @pl.when(hops(sd) == 2)
-                                def _():
-                                    pieces(sd)
+                    pass_on(3, k)
 
             @pl.when(kind > 0)
             def _():
                 block_wait(slot)
 
-            @pl.when((kind == 1) | ((kind == 0) & (i > 0)))
+            @pl.when((kind == 1) | ((kind == 0) & (i > 1)))
             def _():
                 to_sib(slot, 4 * kind + i).start()
 
@@ -322,6 +351,7 @@
     def end_of(i):
         return (x + 2 + i + i // 2 - 2 * (i // 3)) % 4
 
+    pl.semaphore_wait(near, 7)
     targets = (far, up, down)
     for n, row in enumerate(targets):
         last(n, row)
@@ -473,6 +503,7 @@
             dma((16,)), dma((4, 4)), dma((4,)), dma((4,)), dma((8,)),
             dma((4,)), dma((16,)), dma, dma((4,)), dma((16,)), dma,
             dma((3, 4)), dma((3, 4)), dma((8,)), dma((8,)), dma,
+            pltpu.SemaphoreType.REGULAR,
         ],
         compiler_params=pltpu.CompilerParams(
             collective_id=0, has_side_effects=True, vmem_limit_bytes=62 * 1024 * 1024

time: 109 us -> 105 us (0.963)
  the two profiles are of different devices: /device:TPU:69 before, /device:TPU:5 now
where the time goes in v3:
time: 105 us
  Pallas kernels  99.7 us (95%)
  local copies, waits for them, and re-layouts  4.61 us (4%)
    pallas_call x1, Pallas kernels, grow(): pl.pallas_call(kernel, out_shape=[jax.ShapeDtypeStruct(left_env.shape, F3...  99.7 us
    unnamed x2, local copies, waits for them, and re-layouts  4.61 us

profile of v3, /device:TPU:5, one launch (start us, length us, event | category | flops | bytes accessed | tf_op | source)
XLA Modules:
  0.0 105.0 jit_solution(15387609901961208743)
XLA Ops:
  0.6 99.7 %shard_map.77 = (f32[1,32,16,512]{3,2,1,0:T(8,128)}, f32[1,32,16,512]{3,2,1,0:T(8,128)}) custom-call(f32[1,32,16,512]{3,2,1,0:T(8,128)} %le.1, f32[1,32,16,512]{3,2,1,0:T(8,128)} %re.1, f32[1,512,4,512]{3,2,1,0:T(4,128)} %ls.1, f32[1,512,4,512]{3,2,1,0:T(4,128)} %rs.1, f32[16,4,4,16]{3,2,1,0:T(4,128)} %bitcast.6, f32[16,4,4,16]{3,2,1,0:T(4,128)} %bitcast.7), custom_call_target="tpu_custom_call" | custom-call | tf_op jit(solution)/shard_map/pallas_call | solution.py:482
  100.4 2.3 %copy.10 = f32[1,32,16,512]{3,2,1,0:T(8,128)} copy(f32[1,32,16,512]{3,2,1,0:T(8,128)} %get-tuple-element.4) | data formatting | bytes 2097152
  102.7 2.3 %copy.11 = f32[1,32,16,512]{3,2,1,0:T(8,128)} copy(f32[1,32,16,512]{3,2,1,0:T(8,128)} %get-tuple-element.5) | data formatting | bytes 2097152

commit v4 on v3

--- a/solution.py
+++ b/solution.py
@@ -64,44 +64,38 @@
 
     pl.semaphore_wait(barrier, 10 + 2 * jnp.where(above, 1, 0) + 2 * jnp.where(below, 1, 0))
 
-    def x_copy(sd, h, lo, count, sem):
-        env = (le, re)[sd]
-        return pltpu.make_async_remote_copy(
-            src_ref=env.at[0, pl.ds(16 * h + lo, count)],
-            dst_ref=buf.at[4 * h + x, pl.ds(lo, count)],
+    def x_copy(sd, h, k):
+        return pltpu.make_async_remote_copy(
+            src_ref=(le, re)[sd].at[0, pl.ds(16 * h + 2 * k, 2)],
+            dst_ref=buf.at[4 * h + k // 2, pl.ds(4 * x + 2 * (k % 2), 2)],
             send_sem=xsem.at[2 * sd + h],
-            recv_sem=xrcv.at[x, sem],
+            recv_sem=xrcv.at[x, k],
             device_id=dev(z, h, y, 2 * sd + core),
             device_id_type=MESH,
         )
 
-    def hops(sd):
-        return (2 * sd + core + 4 - x) % 4
-
-    def pieces(sd):
-        for k in range(4):
+    def is_local(sd, h):
+        return (2 * sd + core == x) & (core == h)
+
+    def x_start(k, c):
+        for sd in (0, 1):
             for h in (0, 1):
-                x_copy(sd, h, 4 * k, 4, k).start()
-
-    for sd in (0, 1):
-
-        @pl.when(hops(sd) % 2 == 1)
-        def _():
-            pieces(sd)
-
-        @pl.when(hops(sd) == 0)
-        def _():
-            for h in (0, 1):
-
-                @pl.when(core == h)
+
+                @pl.when(is_local(sd, h))
                 def _():
                     pltpu.make_async_copy(
-                        (le, re)[sd].at[0, pl.ds(16 * h, 16)], buf.at[4 * h + x], xrcv.at[x, 0]
+                        (le, re)[sd].at[0, pl.ds(16 * h + 2 * k, 2)],
+                        buf.at[4 * h + k // 2, pl.ds(4 * x + 2 * (k % 2), 2)],
+                        xrcv.at[x, k],
                     ).start()
 
-                @pl.when(core != h)
+                @pl.when(jnp.logical_not(is_local(sd, h)))
                 def _():
-                    x_copy(sd, h, 0, 16, 0).start()
+                    x_copy(sd, h, k).start()
+
+        return c
+
+    lax.fori_loop(0, 8, x_start, 0)
 
     def tell(n, c):
         there = dev(z, (core + n // 4) % 2, y, (x + n % 4) % 4)
@@ -117,10 +111,10 @@
         def _():
             pltpu.make_async_copy((le, re)[sd].at[0], kept, ksem).start()
 
-    def row_of(slot):
-        grp, xx = slot // 4, slot % 4
+    def row_of(unit, xx):
+        grp, k = unit // 4, unit % 4
         yy = (y + grp // 2 + 2 * (grp // 3)) % 4
-        return 128 * yy + 32 * xx + 16 * (grp % 2)
+        return 128 * yy + 32 * xx + 16 * (grp % 2) + 4 * k
 
     def a1_src(t_site, t, c):
         return t_site.at[0, :, t, pl.ds(pl.multiple_of(e_half + 128 * c, 128), 128)]
@@ -132,10 +126,11 @@
             device_id=dev(z, sib, y, x), device_id_type=MESH,
         )
 
-    def a2_copy(t_site, slot):
-        return pltpu.make_async_remote_copy(
-            src_ref=t_site.at[0, pl.ds(row_of(slot), 16)], dst_ref=a2f.at[slot],
-            send_sem=a2snd.at[slot], recv_sem=a2sem.at[slot],
+    def a2_copy(t_site, unit, xx):
+        return pltpu.make_async_remote_copy(
+            src_ref=t_site.at[0, pl.ds(row_of(unit, xx), 4)],
+            dst_ref=a2f.at[unit, pl.ds(4 * xx, 4)],
+            send_sem=a2snd.at[unit], recv_sem=a2sem.at[unit],
             device_id=dev(z, sib, y, x), device_id_type=MESH,
         )
 
@@ -166,50 +161,43 @@
             device_id=dev(z, sib, y, x), device_id_type=MESH,
         )
 
-    def to_row(xx, lo, count):
-        return pltpu.make_async_remote_copy(
-            src_ref=buf.at[4 * core + xx, pl.ds(lo, count)],
-            dst_ref=buf.at[8 + 4 * core + xx, pl.ds(lo, count)],
-            send_sem=ysem.at[xx], recv_sem=rsem.at[8 + 4 * core + xx],
+    def to_row(xx, k):
+        at, unit = pl.ds(4 * xx + 2 * (k % 2), 2), 4 * core + k // 2
+        return pltpu.make_async_remote_copy(
+            src_ref=buf.at[unit, at], dst_ref=buf.at[8 + unit, at],
+            send_sem=ysem.at[k // 2], recv_sem=rsem.at[8 + unit],
             device_id=dev(z, core, (y + 3 + 2 * core) % 4, x), device_id_type=MESH,
         )
 
-    def x_wait(xx, lo, count, sem):
-        at = buf.at[4 * core + xx, pl.ds(lo, count)]
-        pltpu.make_async_copy(at, at, xrcv.at[xx, sem]).wait()
+    def pass_on(xx, k):
+        at = buf.at[4 * core + k // 2, pl.ds(4 * xx + 2 * (k % 2), 2)]
+        pltpu.make_async_copy(at, at, xrcv.at[xx, k]).wait()
+        to_row(xx, k).start()
 
     def col_of(i):
         return (x + i + i // 2 - 2 * (i // 3)) % 4
 
-    x_wait(x, 0, 16, 0)
-    to_row(x, 0, 16).start()
-    to_sib(4 * core + x, 0).start()
+    def own(k, c):
+        pass_on(x, k)
+        return c
+
+    lax.fori_loop(0, 8, own, 0)
     for sd in (0, 1):
         t_site = (ls, rs)[sd]
 
         @pl.when(owner & (side == sd))
         def _():
-            def rows(slot, c):
+            def rows(n, c):
+                unit, xx = n // 4, n % 4
                 pltpu.make_async_copy(
-                    t_site.at[0, pl.ds(row_of(slot), 16)], a2f.at[slot], a2sem.at[slot]
+                    t_site.at[0, pl.ds(row_of(unit, xx), 4)],
+                    a2f.at[unit, pl.ds(4 * xx, 4)],
+                    a2sem.at[unit],
                 ).start()
-                a2_copy(t_site, slot).start()
+                a2_copy(t_site, unit, xx).start()
                 return c
 
-            lax.fori_loop(0, 16, rows, 0)
-
-    def pass_on(i, k):
-        x_wait(col_of(i), 4 * k, 4, k)
-        to_row(col_of(i), 4 * k, 4).start()
-
-    def start_far():
-        for sd in (0, 1):
-
-            @pl.when(hops(sd) == 2)
-            def _():
-                pieces(sd)
-
-    pass_on(1, 0)
+            lax.fori_loop(0, 64, rows, 0)
 
     pltpu.make_async_copy(mpo, mpo, mposem).wait()
     small = split(mpo[...].reshape(256, 16))
@@ -242,17 +230,10 @@
             out = jnp.dot(move, wide, preferred_element_type=F32)
             ref[...] = jnp.where(diagonal, out, 0.0).astype(BF16)
 
-    pass_on(1, 1)
     for t in range(4):
         pltpu.make_async_copy(a1f.at[t], a1f.at[t], a1sem.at[t]).wait()
         a1h[:, 128 * t : 128 * (t + 1)], a1l[:, 128 * t : 128 * (t + 1)] = split(a1f[t])
 
-    pass_on(1, 2)
-    pass_on(1, 3)
-    start_far()
-    to_sib(4 * core + col_of(1), 1).start()
-    for k in range(4):
-        pass_on(2, k)
 
     def turn(n, c):
         for k in (0, 1):
@@ -294,38 +275,36 @@
                 ql[at, 128 * v : 128 * v + 128] = ol[rows, cols]
 
     def step(n, c):
-        kind = n % 4
-        i = n // 4 - (kind + 1) // 2
-
-        @pl.when((i >= 0) & (i < 4))
-        def _():
-            xx = col_of(i)
-            from_sib = kind // 2
-            grp = (1 - from_sib) * (core + 2 * kind) + from_sib * (sib + 2 * (kind - 2))
-            slot = 4 * grp + xx
-
-            @pl.when((kind == 0) & (i == 3))
+        group, kind = n // 4, n % 4
+        k = group - 1 + kind // 2
+        unit = 4 * (2 - 2 * (kind // 2) + (kind % 2) * sib + (1 - kind % 2) * core) + k
+
+        for i in range(3):
+
+            @pl.when((kind == i) & (group < 4))
             def _():
-                for k in range(4):
-                    pass_on(3, k)
-
-            @pl.when(kind > 0)
+                for m in (2 * i, 2 * i + 1):
+                    pass_on(col_of(m % 3 + 1), 2 * group + m // 3)
+
+        @pl.when((k >= 0) & (k < 4))
+        def _():
+            @pl.when(kind != 2)
             def _():
-                block_wait(slot)
-
-            @pl.when((kind == 1) | ((kind == 0) & (i > 1)))
+                block_wait(unit)
+
+            @pl.when(kind % 2 == 0)
             def _():
-                to_sib(slot, 4 * kind + i).start()
-
-            first_two(slot)
-
-        @pl.when(n == 0)
+                to_sib(unit, 4 * (1 - kind // 2) + k).start()
+
+            first_two(unit)
+
+        @pl.when(n == 3)
         def _():
             lax.fori_loop(0, 8, turn, 0)
 
         return c
 
-    lax.fori_loop(0, 24, step, 0)
+    lax.fori_loop(0, 18, step, 0)
 
     def last(n, row):
         lhs = pl.ds(pl.multiple_of(128 * row, 128), 128)
@@ -340,51 +319,51 @@
 
         lax.fori_loop(0, 8, cols, 0)
 
-    def part_copy(n, row, i):
-        at = pl.ds(32 * end_of(i), 32)
+    def rows_of(q):
+        i = q // 2
+        return pl.ds(32 * ((x + 2 + i + i // 2 - 2 * (i // 3)) % 4) + 16 * (q % 2), 16)
+
+    def part_copy(n, row, q):
+        at = rows_of(q)
         return pltpu.make_async_remote_copy(
             src_ref=part.at[n, at], dst_ref=rcv.at[n, at],
-            send_sem=psnd.at[n, i], recv_sem=prcv.at[n, i],
+            send_sem=psnd.at[n, q], recv_sem=prcv.at[n, q],
             device_id=dev(z, core, row, x), device_id_type=MESH,
         )
-
-    def end_of(i):
-        return (x + 2 + i + i // 2 - 2 * (i // 3)) % 4
 
     pl.semaphore_wait(near, 7)
     targets = (far, up, down)
     for n, row in enumerate(targets):
         last(n, row)
-        for i in range(4):
-            part_copy(n, row, i).start()
+
+        def send(q, c):
+            part_copy(n, row, q).start()
+            return c
+
+        lax.fori_loop(0, 8, send, 0)
     last(3, y)
 
     segment = 2 * z + x % 2
     target = segment + 1 - 2 * side
     valid = (target >= 0) & (target < 8)
 
-    def out_copy(sd, n, xx):
-        src = (part.at[3], rcv.at[1])[n]
+    def ends(sd, n, q):
+        i = q // 2
         half = (y % 2) if n == 0 else 1 - y % 2
         lanes = pl.ds(pl.multiple_of(256 * half + 128 * core, 128), 128)
-        out = (nl, nr)[sd]
-        return pltpu.make_async_remote_copy(
-            src_ref=src.at[pl.ds(32 * xx, 32)], dst_ref=out.at[0, :, :, lanes],
-            send_sem=osnd.at[4 * n + xx], recv_sem=orcv.at[4 * sd + 2 * n + core],
+        src = (part.at[3], rcv.at[1])[n].at[rows_of(q)]
+        dst = (nl, nr)[sd].at[0, pl.ds(16 * (q % 2), 16), :, lanes]
+        return src, dst, orcv.at[4 * sd + 2 * n + core], (x + 2 + i + i // 2 - 2 * (i // 3)) % 4
+
+    def out_copy(sd, n, q):
+        src, dst, sem, xx = ends(sd, n, q)
+        return pltpu.make_async_remote_copy(
+            src_ref=src, dst_ref=dst, send_sem=osnd.at[8 * n + q], recv_sem=sem,
             device_id=(target, 4 * y + xx), device_id_type=MESH,
         )
 
-    def out_local(sd, n):
-        src = (part.at[3], rcv.at[1])[n]
-        half = (y % 2) if n == 0 else 1 - y % 2
-        lanes = pl.ds(pl.multiple_of(256 * half + 128 * core, 128), 128)
-        out = (nl, nr)[sd]
-        return pltpu.make_async_copy(
-            src.at[pl.ds(32 * x, 32)], out.at[0, :, :, lanes], orcv.at[4 * sd + 2 * n + core]
-        )
-
-    def hand_off(n, xx, wait):
-        local = (xx == x) & (target == site)
+    def hand_off(n, q, wait):
+        local = (q // 2 == 3) & (target == site)
         for sd in (0, 1):
 
             @pl.when(valid & (side == sd))
@@ -392,15 +371,16 @@
                 @pl.when(jnp.logical_not(local))
                 def _():
                     if wait:
-                        out_copy(sd, n, xx).wait_send()
+                        out_copy(sd, n, q).wait_send()
                     else:
-                        out_copy(sd, n, xx).start()
+                        out_copy(sd, n, q).start()
 
                 if not wait:
 
                     @pl.when(local)
                     def _():
-                        out_local(sd, n).start()
+                        src, dst, sem, _ = ends(sd, n, q)
+                        pltpu.make_async_copy(src, dst, sem).start()
 
     for sd in (0, 1):
 
@@ -409,37 +389,44 @@
             pltpu.make_async_copy((le, re)[sd].at[0], kept, ksem).wait()
             pltpu.make_async_copy(kept, (nl, nr)[sd].at[0], ksem).start()
 
-    def finish(n, xx):
-        def add(k, c):
-            at = pl.ds(32 * xx + 8 * k, 8)
-            if n == 0:
-                part[3, at] = part[3, at] + rcv[0, at]
-            else:
-                rcv[1, at] = rcv[1, at] + rcv[2, at]
-            return c
-
-        lax.fori_loop(0, 4, add, 0)
-        hand_off(n, xx, False)
-
-    for i in range(4):
-        part_copy(0, far, i).wait_recv()
-        finish(0, end_of(i))
-    for i in range(4):
-        part_copy(1, up, i).wait_recv()
-        part_copy(2, down, i).wait_recv()
-        finish(1, end_of(i))
+    def finish_far(q, c):
+        at = rows_of(q)
+        part_copy(0, far, q).wait_recv()
+        part[3, at] = part[3, at] + rcv[0, at]
+        hand_off(0, q, False)
+        return c
+
+    lax.fori_loop(0, 8, finish_far, 0)
+
+    def finish_near(q, c):
+        at = rows_of(q)
+        part_copy(1, up, q).wait_recv()
+        part_copy(2, down, q).wait_recv()
+        rcv[1, at] = rcv[1, at] + rcv[2, at]
+        hand_off(1, q, False)
+        return c
+
+    lax.fori_loop(0, 8, finish_near, 0)
 
     for sd in (0, 1):
         for h in (0, 1):
 
-            @pl.when((hops(sd) != 0) | (core != h))
+            @pl.when(jnp.logical_not(is_local(sd, h)))
             def _():
-                x_copy(sd, h, 0, 16, 0).wait_send()
-
-    for i in range(4):
-        to_row(col_of(i), 0, 16).wait_send()
-        to_sib(4 * core + col_of(i), i).wait_send()
-        to_sib(8 + 4 * core + col_of(i), 4 + i).wait_send()
+                pltpu.make_async_remote_copy(
+                    src_ref=(le, re)[sd].at[0, pl.ds(16 * h, 16)], dst_ref=buf.at[4 * h],
+                    send_sem=xsem.at[2 * sd + h], recv_sem=xrcv.at[x, 0],
+                    device_id=dev(z, h, y, 2 * sd + core), device_id_type=MESH,
+                ).wait_send()
+
+    for k in range(4):
+        pltpu.make_async_remote_copy(
+            src_ref=buf.at[4 * core + k], dst_ref=buf.at[8 + 4 * core + k],
+            send_sem=ysem.at[k], recv_sem=rsem.at[8 + 4 * core + k],
+            device_id=dev(z, core, (y + 3 + 2 * core) % 4, x), device_id_type=MESH,
+        ).wait_send()
+        to_sib(4 * core + k, k).wait_send()
+        to_sib(8 + 4 * core + k, 4 + k).wait_send()
     for sd in (0, 1):
         t_site = (ls, rs)[sd]
 
@@ -449,18 +436,25 @@
                 a1_copy(t_site, t).wait_send()
             mpo_copy(sd).wait_send()
 
-            def rows(slot, c):
-                a2_copy(t_site, slot).wait_send()
+            def rows(unit, c):
+                pltpu.make_async_remote_copy(
+                    src_ref=t_site.at[0, pl.ds(0, 16)], dst_ref=a2f.at[unit],
+                    send_sem=a2snd.at[unit], recv_sem=a2sem.at[unit],
+                    device_id=dev(z, sib, y, x), device_id_type=MESH,
+                ).wait_send()
                 return c
 
             lax.fori_loop(0, 16, rows, 0)
 
-    for n, row in enumerate(targets):
-        for i in range(4):
-            part_copy(n, row, i).wait_send()
-    for i in range(4):
+
+    def sent(q, c):
+        for n, row in enumerate(targets):
+            part_copy(n, row, q).wait_send()
         for n in (0, 1):
-            hand_off(n, end_of(i), True)
+            hand_off(n, q, True)
+        return c
+
+    lax.fori_loop(0, 8, sent, 0)
     for sd in (0, 1):
 
         @pl.when((site > 0) if sd == 0 else (site < 7))
@@ -500,15 +494,20 @@
             vmem((4, 128, 16, 128), F32),
             vmem((3, 128, 16, 128), F32),
             vmem((32, 16, 512), F32),
-            dma((16,)), dma((4, 4)), dma((4,)), dma((4,)), dma((8,)),
+            dma((16,)), dma((4, 8)), dma((4,)), dma((4,)), dma((8,)),
             dma((4,)), dma((16,)), dma, dma((4,)), dma((16,)), dma,
-            dma((3, 4)), dma((3, 4)), dma((8,)), dma((8,)), dma,
+            dma((3, 8)), dma((3, 8)), dma((8,)), dma((16,)), dma,
             pltpu.SemaphoreType.REGULAR,
         ],
         compiler_params=pltpu.CompilerParams(
-            collective_id=0, has_side_effects=True, vmem_limit_bytes=62 * 1024 * 1024
+            collective_id=0, has_side_effects=True, vmem_limit_bytes=40 * 1024 * 1024
         ),
-    )(left_env, right_env, left_site, right_site, left_mpo, right_mpo)
+    )(
+        *(
+            pltpu.with_memory_space_constraint(array, pltpu.HBM)
+            for array in (left_env, right_env, left_site, right_site, left_mpo, right_mpo)
+        )
+    )
 
 
 def local(left_env, right_env, left_site, right_site, left_mpo, right_mpo):

time: 105 us -> 102 us (0.971)
  local copies, waits for them, and re-layouts: 4.61 us -> 1.94 us
    unnamed x2, local copies, waits for them, and re-layouts: 4.61 us -> 1.94 us
where the time goes in v4:
time: 102 us; the launch traced here: 101 us
  Pallas kernels  98.9 us (97%)
  local copies, waits for them, and re-layouts  1.94 us (2%)
    pallas_call x1, Pallas kernels, grow(): pl.pallas_call(kernel, out_shape=[jax.ShapeDtypeStruct(left_env.shape, F3...  98.9 us

profile of v4, /device:TPU:5, one launch (start us, length us, event | category | flops | bytes accessed | tf_op | source)
XLA Modules:
  0.0 101.4 jit_solution(3735322786094068267)
XLA Ops:
  0.6 98.9 %shard_map.77 = (f32[1,32,16,512]{3,2,1,0:T(8,128)S(1)}, f32[1,32,16,512]{3,2,1,0:T(8,128)S(1)}) custom-call(f32[1,32,16,512]{3,2,1,0:T(8,128)} %le.1, f32[1,32,16,512]{3,2,1,0:T(8,128)} %re.1, f32[1,512,4,512]{3,2,1,0:T(4,128)} %ls.1, f32[1,512,4,512]{3,2,1,0:T(4,128)} %rs.1, f32[16,4,4,16]{3,2,1,0:T(4,128)} %bitcast.6, f32[16,4,4,16]{3,2,1,0:T(4,128)} %bitcast.7), custom_call_target="tpu_custom_call" | custom-call | tf_op jit(solution)/shard_map/pallas_call | solution.py:476
  99.5 1.0 copy.10
  100.5 1.0 copy.11

commit v5 on v4

--- a/solution.py
+++ b/solution.py
@@ -8,6 +8,7 @@
 MESH = pl.DeviceIdType.MESH
 F32 = jnp.float32
 BF16 = jnp.bfloat16
+AHEAD = 14
 
 
 def split(value):
@@ -67,7 +68,7 @@
     def x_copy(sd, h, k):
         return pltpu.make_async_remote_copy(
             src_ref=(le, re)[sd].at[0, pl.ds(16 * h + 2 * k, 2)],
-            dst_ref=buf.at[4 * h + k // 2, pl.ds(4 * x + 2 * (k % 2), 2)],
+            dst_ref=buf.at[h + 4 * (k // 2), pl.ds(4 * x + 2 * (k % 2), 2)],
             send_sem=xsem.at[2 * sd + h],
             recv_sem=xrcv.at[x, k],
             device_id=dev(z, h, y, 2 * sd + core),
@@ -85,7 +86,7 @@
                 def _():
                     pltpu.make_async_copy(
                         (le, re)[sd].at[0, pl.ds(16 * h + 2 * k, 2)],
-                        buf.at[4 * h + k // 2, pl.ds(4 * x + 2 * (k % 2), 2)],
+                        buf.at[h + 4 * (k // 2), pl.ds(4 * x + 2 * (k % 2), 2)],
                         xrcv.at[x, k],
                     ).start()
 
@@ -112,7 +113,7 @@
             pltpu.make_async_copy((le, re)[sd].at[0], kept, ksem).start()
 
     def row_of(unit, xx):
-        grp, k = unit // 4, unit % 4
+        grp, k = unit % 4, unit // 4
         yy = (y + grp // 2 + 2 * (grp // 3)) % 4
         return 128 * yy + 32 * xx + 16 * (grp % 2) + 4 * k
 
@@ -162,15 +163,15 @@
         )
 
     def to_row(xx, k):
-        at, unit = pl.ds(4 * xx + 2 * (k % 2), 2), 4 * core + k // 2
-        return pltpu.make_async_remote_copy(
-            src_ref=buf.at[unit, at], dst_ref=buf.at[8 + unit, at],
-            send_sem=ysem.at[k // 2], recv_sem=rsem.at[8 + unit],
+        at, unit = pl.ds(4 * xx + 2 * (k % 2), 2), core + 4 * (k // 2)
+        return pltpu.make_async_remote_copy(
+            src_ref=buf.at[unit, at], dst_ref=buf.at[2 + unit, at],
+            send_sem=ysem.at[k // 2], recv_sem=rsem.at[2 + unit],
             device_id=dev(z, core, (y + 3 + 2 * core) % 4, x), device_id_type=MESH,
         )
 
     def pass_on(xx, k):
-        at = buf.at[4 * core + k // 2, pl.ds(4 * xx + 2 * (k % 2), 2)]
+        at = buf.at[core + 4 * (k // 2), pl.ds(4 * xx + 2 * (k % 2), 2)]
         pltpu.make_async_copy(at, at, xrcv.at[xx, k]).wait()
         to_row(xx, k).start()
 
@@ -274,10 +275,25 @@
                 qh[at, 128 * v : 128 * v + 128] = oh[rows, cols]
                 ql[at, 128 * v : 128 * v + 128] = ol[rows, cols]
 
+    def last(n, row, first, end):
+        lhs, deep = pl.ds(pl.multiple_of(128 * row, 128), 128), slice(first, end)
+        flat = part.reshape(4, 2048, 128)
+
+        def cols(i, c):
+            at = pl.ds(pl.multiple_of(256 * i, 256), 256)
+            out = dot3(a2h[lhs, deep], a2l[lhs, deep], qh[deep, at], ql[deep, at])
+            for k in (0, 1):
+                rows = pl.ds(2 * i + k, 128, stride=16)
+                piece = out[:, 128 * k : 128 * k + 128]
+                flat[n, rows, :] = piece if first == 0 else flat[n, rows, :] + piece
+            return c
+
+        lax.fori_loop(0, 8, cols, 0)
+
     def step(n, c):
         group, kind = n // 4, n % 4
         k = group - 1 + kind // 2
-        unit = 4 * (2 - 2 * (kind // 2) + (kind % 2) * sib + (1 - kind % 2) * core) + k
+        unit = 4 * k + 2 - 2 * (kind // 2) + (kind % 2) * sib + (1 - kind % 2) * core
 
         for i in range(3):
 
@@ -302,26 +318,17 @@
         def _():
             lax.fori_loop(0, 8, turn, 0)
 
+        @pl.when(n == AHEAD)
+        def _():
+            last(0, far, 0, 768)
+
         return c
 
     lax.fori_loop(0, 18, step, 0)
 
-    def last(n, row):
-        lhs = pl.ds(pl.multiple_of(128 * row, 128), 128)
-        flat = part.reshape(4, 2048, 128)
-
-        def cols(i, c):
-            at = pl.ds(pl.multiple_of(256 * i, 256), 256)
-            out = dot3(a2h[lhs, :], a2l[lhs, :], qh[:, at], ql[:, at])
-            for k in (0, 1):
-                flat[n, pl.ds(2 * i + k, 128, stride=16), :] = out[:, 128 * k : 128 * k + 128]
-            return c
-
-        lax.fori_loop(0, 8, cols, 0)
-
     def rows_of(q):
-        i = q // 2
-        return pl.ds(32 * ((x + 2 + i + i // 2 - 2 * (i // 3)) % 4) + 16 * (q % 2), 16)
+        i = q // 4
+        return pl.ds(32 * ((x + 2 + i + i // 2 - 2 * (i // 3)) % 4) + 8 * (q % 4), 8)
 
     def part_copy(n, row, q):
         at = rows_of(q)
@@ -334,36 +341,36 @@
     pl.semaphore_wait(near, 7)
     targets = (far, up, down)
     for n, row in enumerate(targets):
-        last(n, row)
+        last(n, row, 768 if n == 0 else 0, 1024)
 
         def send(q, c):
             part_copy(n, row, q).start()
             return c
 
-        lax.fori_loop(0, 8, send, 0)
-    last(3, y)
+        lax.fori_loop(0, 16, send, 0)
+    last(3, y, 0, 1024)
 
     segment = 2 * z + x % 2
     target = segment + 1 - 2 * side
     valid = (target >= 0) & (target < 8)
 
     def ends(sd, n, q):
-        i = q // 2
+        i = q // 4
         half = (y % 2) if n == 0 else 1 - y % 2
         lanes = pl.ds(pl.multiple_of(256 * half + 128 * core, 128), 128)
         src = (part.at[3], rcv.at[1])[n].at[rows_of(q)]
-        dst = (nl, nr)[sd].at[0, pl.ds(16 * (q % 2), 16), :, lanes]
+        dst = (nl, nr)[sd].at[0, pl.ds(8 * (q % 4), 8), :, lanes]
         return src, dst, orcv.at[4 * sd + 2 * n + core], (x + 2 + i + i // 2 - 2 * (i // 3)) % 4
 
     def out_copy(sd, n, q):
         src, dst, sem, xx = ends(sd, n, q)
         return pltpu.make_async_remote_copy(
-            src_ref=src, dst_ref=dst, send_sem=osnd.at[8 * n + q], recv_sem=sem,
+            src_ref=src, dst_ref=dst, send_sem=osnd.at[16 * n + q], recv_sem=sem,
             device_id=(target, 4 * y + xx), device_id_type=MESH,
         )
 
     def hand_off(n, q, wait):
-        local = (q // 2 == 3) & (target == site)
+        local = (q // 4 == 3) & (target == site)
         for sd in (0, 1):
 
             @pl.when(valid & (side == sd))
@@ -396,7 +403,7 @@
         hand_off(0, q, False)
         return c
 
-    lax.fori_loop(0, 8, finish_far, 0)
+    lax.fori_loop(0, 16, finish_far, 0)
 
     def finish_near(q, c):
         at = rows_of(q)
@@ -406,7 +413,7 @@
         hand_off(1, q, False)
         return c
 
-    lax.fori_loop(0, 8, finish_near, 0)
+    lax.fori_loop(0, 16, finish_near, 0)
 
     for sd in (0, 1):
         for h in (0, 1):
@@ -421,12 +428,12 @@
 
     for k in range(4):
         pltpu.make_async_remote_copy(
-            src_ref=buf.at[4 * core + k], dst_ref=buf.at[8 + 4 * core + k],
-            send_sem=ysem.at[k], recv_sem=rsem.at[8 + 4 * core + k],
+            src_ref=buf.at[4 * k + core], dst_ref=buf.at[4 * k + 2 + core],
+            send_sem=ysem.at[k], recv_sem=rsem.at[4 * k + 2 + core],
             device_id=dev(z, core, (y + 3 + 2 * core) % 4, x), device_id_type=MESH,
         ).wait_send()
-        to_sib(4 * core + k, k).wait_send()
-        to_sib(8 + 4 * core + k, 4 + k).wait_send()
+        to_sib(4 * k + core, k).wait_send()
+        to_sib(4 * k + 2 + core, 4 + k).wait_send()
     for sd in (0, 1):
         t_site = (ls, rs)[sd]
 
@@ -454,7 +461,7 @@
             hand_off(n, q, True)
         return c
 
-    lax.fori_loop(0, 8, sent, 0)
+    lax.fori_loop(0, 16, sent, 0)
     for sd in (0, 1):
 
         @pl.when((site > 0) if sd == 0 else (site < 7))
@@ -496,7 +503,7 @@
             vmem((32, 16, 512), F32),
             dma((16,)), dma((4, 8)), dma((4,)), dma((4,)), dma((8,)),
             dma((4,)), dma((16,)), dma, dma((4,)), dma((16,)), dma,
-            dma((3, 8)), dma((3, 8)), dma((8,)), dma((16,)), dma,
+            dma((3, 16)), dma((3, 16)), dma((8,)), dma((32,)), dma,
             pltpu.SemaphoreType.REGULAR,
         ],
         compiler_params=pltpu.CompilerParams(

time: 102 us -> 100 us (0.980)
  Pallas kernels: 98.9 us -> 97.4 us
    pallas_call x1, Pallas kernels: 98.9 us -> 97.4 us  [grow(): pl.pallas_call(kernel, out_shape=[jax.ShapeDtypeStruct(left_env.shape, F3...]
where the time goes in v5:
time: 100 us
  Pallas kernels  97.4 us (97%)
  local copies, waits for them, and re-layouts  1.94 us (2%)
    pallas_call x1, Pallas kernels, grow(): pl.pallas_call(kernel, out_shape=[jax.ShapeDtypeStruct(left_env.shape, F3...  97.4 us

profile of v5, /device:TPU:5, one launch (start us, length us, event | category | flops | bytes accessed | tf_op | source)
XLA Modules:
  0.0 100.0 jit_solution(16235012292644272475)
XLA Ops:
  0.6 97.4 %shard_map.77 = (f32[1,32,16,512]{3,2,1,0:T(8,128)S(1)}, f32[1,32,16,512]{3,2,1,0:T(8,128)S(1)}) custom-call(f32[1,32,16,512]{3,2,1,0:T(8,128)} %le.1, f32[1,32,16,512]{3,2,1,0:T(8,128)} %re.1, f32[1,512,4,512]{3,2,1,0:T(4,128)} %ls.1, f32[1,512,4,512]{3,2,1,0:T(4,128)} %rs.1, f32[16,4,4,16]{3,2,1,0:T(4,128)} %bitcast.6, f32[16,4,4,16]{3,2,1,0:T(4,128)} %bitcast.7), custom_call_target="tpu_custom_call" | custom-call | tf_op jit(solution)/shard_map/pallas_call | solution.py:483
  98.1 1.0 copy.10
  99.0 1.0 copy.11

commit v6 on v5

--- a/solution.py
+++ b/solution.py
@@ -334,7 +334,7 @@
         at = rows_of(q)
         return pltpu.make_async_remote_copy(
             src_ref=part.at[n, at], dst_ref=rcv.at[n, at],
-            send_sem=psnd.at[n, q], recv_sem=prcv.at[n, q],
+            send_sem=psnd.at[n], recv_sem=prcv.at[n, q],
             device_id=dev(z, core, row, x), device_id_type=MESH,
         )
 
@@ -365,11 +365,11 @@
     def out_copy(sd, n, q):
         src, dst, sem, xx = ends(sd, n, q)
         return pltpu.make_async_remote_copy(
-            src_ref=src, dst_ref=dst, send_sem=osnd.at[16 * n + q], recv_sem=sem,
+            src_ref=src, dst_ref=dst, send_sem=osnd.at[4 * n + q // 4], recv_sem=sem,
             device_id=(target, 4 * y + xx), device_id_type=MESH,
         )
 
-    def hand_off(n, q, wait):
+    def hand_off(n, q):
         local = (q // 4 == 3) & (target == site)
         for sd in (0, 1):
 
@@ -377,17 +377,12 @@
             def _():
                 @pl.when(jnp.logical_not(local))
                 def _():
-                    if wait:
-                        out_copy(sd, n, q).wait_send()
-                    else:
-                        out_copy(sd, n, q).start()
-
-                if not wait:
-
-                    @pl.when(local)
-                    def _():
-                        src, dst, sem, _ = ends(sd, n, q)
-                        pltpu.make_async_copy(src, dst, sem).start()
+                    out_copy(sd, n, q).start()
+
+                @pl.when(local)
+                def _():
+                    src, dst, sem, _ = ends(sd, n, q)
+                    pltpu.make_async_copy(src, dst, sem).start()
 
     for sd in (0, 1):
 
@@ -395,25 +390,6 @@
         def _():
             pltpu.make_async_copy((le, re)[sd].at[0], kept, ksem).wait()
             pltpu.make_async_copy(kept, (nl, nr)[sd].at[0], ksem).start()
-
-    def finish_far(q, c):
-        at = rows_of(q)
-        part_copy(0, far, q).wait_recv()
-        part[3, at] = part[3, at] + rcv[0, at]
-        hand_off(0, q, False)
-        return c
-
-    lax.fori_loop(0, 16, finish_far, 0)
-
-    def finish_near(q, c):
-        at = rows_of(q)
-        part_copy(1, up, q).wait_recv()
-        part_copy(2, down, q).wait_recv()
-        rcv[1, at] = rcv[1, at] + rcv[2, at]
-        hand_off(1, q, False)
-        return c
-
-    lax.fori_loop(0, 16, finish_near, 0)
 
     for sd in (0, 1):
         for h in (0, 1):
@@ -453,15 +429,43 @@
 
             lax.fori_loop(0, 16, rows, 0)
 
-
-    def sent(q, c):
-        for n, row in enumerate(targets):
-            part_copy(n, row, q).wait_send()
+    def finish_far(q, c):
+        at = rows_of(q)
+        part_copy(0, far, q).wait_recv()
+        part[3, at] = part[3, at] + rcv[0, at]
+        hand_off(0, q)
+        return c
+
+    lax.fori_loop(0, 16, finish_far, 0)
+
+    def finish_near(q, c):
+        at = rows_of(q)
+        part_copy(1, up, q).wait_recv()
+        part_copy(2, down, q).wait_recv()
+        rcv[1, at] = rcv[1, at] + rcv[2, at]
+        hand_off(1, q)
+        return c
+
+    lax.fori_loop(0, 16, finish_near, 0)
+
+
+    for n, row in enumerate(targets):
+        pltpu.make_async_remote_copy(
+            src_ref=part.at[n], dst_ref=rcv.at[n], send_sem=psnd.at[n], recv_sem=prcv.at[n, 0],
+            device_id=dev(z, core, row, x), device_id_type=MESH,
+        ).wait_send()
+
+    for i in range(4):
         for n in (0, 1):
-            hand_off(n, q, True)
-        return c
-
-    lax.fori_loop(0, 16, sent, 0)
+
+            @pl.when(valid & ((target != site) | (i < 3)))
+            def _():
+                pltpu.make_async_remote_copy(
+                    src_ref=part.at[3, pl.ds(0, 32)], dst_ref=nl.at[0, :, :, pl.ds(0, 128)],
+                    send_sem=osnd.at[4 * n + i], recv_sem=orcv.at[0],
+                    device_id=dev(z, sib, y, x), device_id_type=MESH,
+                ).wait_send()
+
     for sd in (0, 1):
 
         @pl.when((site > 0) if sd == 0 else (site < 7))
@@ -503,7 +507,7 @@
             vmem((32, 16, 512), F32),
             dma((16,)), dma((4, 8)), dma((4,)), dma((4,)), dma((8,)),
             dma((4,)), dma((16,)), dma, dma((4,)), dma((16,)), dma,
-            dma((3, 16)), dma((3, 16)), dma((8,)), dma((32,)), dma,
+            dma((3, 16)), dma((3,)), dma((8,)), dma((8,)), dma,
             pltpu.SemaphoreType.REGULAR,
         ],
         compiler_params=pltpu.CompilerParams(

time: 100 us -> 99.5 us (level)
  no operation moved by 1% of the time
where the time goes in v6:
time: 99.5 us; the launch traced here: 99.4 us
  Pallas kernels  96.8 us (97%)
  local copies, waits for them, and re-layouts  1.94 us (2%)
    pallas_call x1, Pallas kernels, grow(): pl.pallas_call(kernel, out_shape=[jax.ShapeDtypeStruct(left_env.shape, F3...  96.8 us

profile of v6, /device:TPU:5, one launch (start us, length us, event | category | flops | bytes accessed | tf_op | source)
XLA Modules:
  0.0 99.4 jit_solution(15637263025394184203)
XLA Ops:
  0.6 96.8 %shard_map.77 = (f32[1,32,16,512]{3,2,1,0:T(8,128)S(1)}, f32[1,32,16,512]{3,2,1,0:T(8,128)S(1)}) custom-call(f32[1,32,16,512]{3,2,1,0:T(8,128)} %le.1, f32[1,32,16,512]{3,2,1,0:T(8,128)} %re.1, f32[1,512,4,512]{3,2,1,0:T(4,128)} %ls.1, f32[1,512,4,512]{3,2,1,0:T(4,128)} %rs.1, f32[16,4,4,16]{3,2,1,0:T(4,128)} %bitcast.6, f32[16,4,4,16]{3,2,1,0:T(4,128)} %bitcast.7), custom_call_target="tpu_custom_call" | custom-call | tf_op jit(solution)/shard_map/pallas_call | solution.py:487
  97.4 1.0 copy.10
  98.4 1.0 copy.11

commit v7 on v6

--- a/solution.py
+++ b/solution.py
@@ -280,15 +280,15 @@
         flat = part.reshape(4, 2048, 128)
 
         def cols(i, c):
-            at = pl.ds(pl.multiple_of(256 * i, 256), 256)
+            at = pl.ds(pl.multiple_of(1024 * i, 1024), 1024)
             out = dot3(a2h[lhs, deep], a2l[lhs, deep], qh[deep, at], ql[deep, at])
-            for k in (0, 1):
-                rows = pl.ds(2 * i + k, 128, stride=16)
+            for k in range(8):
+                rows = pl.ds(8 * i + k, 128, stride=16)
                 piece = out[:, 128 * k : 128 * k + 128]
                 flat[n, rows, :] = piece if first == 0 else flat[n, rows, :] + piece
             return c
 
-        lax.fori_loop(0, 8, cols, 0)
+        lax.fori_loop(0, 2, cols, 0)
 
     def step(n, c):
         group, kind = n // 4, n % 4

time: 99.5 us -> 98 us (0.985)
  Pallas kernels: 96.8 us -> 95.3 us
    pallas_call x1, Pallas kernels: 96.8 us -> 95.3 us  [grow(): pl.pallas_call(kernel, out_shape=[jax.ShapeDtypeStruct(left_env.shape, F3...]
where the time goes in v7:
time: 98 us; the launch traced here: 97.9 us
  Pallas kernels  95.3 us (97%)
  local copies, waits for them, and re-layouts  1.94 us (2%)
    pallas_call x1, Pallas kernels, grow(): pl.pallas_call(kernel, out_shape=[jax.ShapeDtypeStruct(left_env.shape, F3...  95.3 us

profile of v7, /device:TPU:5, one launch (start us, length us, event | category | flops | bytes accessed | tf_op | source)
XLA Modules:
  0.0 97.9 jit_solution(8364786333768448953)
XLA Ops:
  0.6 95.3 %shard_map.77 = (f32[1,32,16,512]{3,2,1,0:T(8,128)S(1)}, f32[1,32,16,512]{3,2,1,0:T(8,128)S(1)}) custom-call(f32[1,32,16,512]{3,2,1,0:T(8,128)} %le.1, f32[1,32,16,512]{3,2,1,0:T(8,128)} %re.1, f32[1,512,4,512]{3,2,1,0:T(4,128)} %ls.1, f32[1,512,4,512]{3,2,1,0:T(4,128)} %rs.1, f32[16,4,4,16]{3,2,1,0:T(4,128)} %bitcast.6, f32[16,4,4,16]{3,2,1,0:T(4,128)} %bitcast.7), custom_call_target="tpu_custom_call" | custom-call | tf_op jit(solution)/shard_map/pallas_call | solution.py:487
  95.9 1.0 copy.10
  96.9 1.0 copy.11

commit v8 on v7

--- a/solution.py
+++ b/solution.py
@@ -8,7 +8,7 @@
 MESH = pl.DeviceIdType.MESH
 F32 = jnp.float32
 BF16 = jnp.bfloat16
-AHEAD = 14
+AHEAD = 15
 
 
 def split(value):
@@ -17,10 +17,9 @@
 
 
 def dot3(ah, al, bh, bl):
-    out = jnp.dot(ah, bh, preferred_element_type=F32)
-    out += jnp.dot(ah, bl, preferred_element_type=F32)
-    out += jnp.dot(al, bh, preferred_element_type=F32)
-    return out
+    left = jnp.concatenate([ah, ah, al], axis=1)
+    right = jnp.concatenate([bh, bl, bh], axis=0)
+    return jnp.dot(left, right, preferred_element_type=F32)
 
 
 def kernel(

time: 98 us -> 98.3 us (level)
  no operation moved by 1% of the time
where the time goes in v8:
time: 98.3 us; the launch traced here: 98.2 us
  Pallas kernels  95.6 us (97%)
  local copies, waits for them, and re-layouts  1.94 us (2%)
    pallas_call x1, Pallas kernels, grow(): pl.pallas_call(kernel, out_shape=[jax.ShapeDtypeStruct(left_env.shape, F3...  95.6 us

profile of v8, /device:TPU:5, one launch (start us, length us, event | category | flops | bytes accessed | tf_op | source)
XLA Modules:
  0.0 98.2 jit_solution(80265206214424571)
XLA Ops:
  0.6 95.6 %shard_map.77 = (f32[1,32,16,512]{3,2,1,0:T(8,128)S(1)}, f32[1,32,16,512]{3,2,1,0:T(8,128)S(1)}) custom-call(f32[1,32,16,512]{3,2,1,0:T(8,128)} %le.1, f32[1,32,16,512]{3,2,1,0:T(8,128)} %re.1, f32[1,512,4,512]{3,2,1,0:T(4,128)} %ls.1, f32[1,512,4,512]{3,2,1,0:T(4,128)} %rs.1, f32[16,4,4,16]{3,2,1,0:T(4,128)} %bitcast.6, f32[16,4,4,16]{3,2,1,0:T(4,128)} %bitcast.7), custom_call_target="tpu_custom_call" | custom-call | tf_op jit(solution)/shard_map/pallas_call | solution.py:486
  96.2 1.0 copy.10
  97.2 1.0 copy.11

commit v9 on v7

--- a/solution.py
+++ b/solution.py
@@ -8,7 +8,7 @@
 MESH = pl.DeviceIdType.MESH
 F32 = jnp.float32
 BF16 = jnp.bfloat16
-AHEAD = 14
+AHEAD = 15
 
 
 def split(value):

time: 98 us -> 98.3 us (level)
  no operation moved by 1% of the time
where the time goes in v9:
time: 98.3 us; the launch traced here: 98.1 us
  Pallas kernels  95.6 us (97%)
  local copies, waits for them, and re-layouts  1.94 us (2%)
    pallas_call x1, Pallas kernels, grow(): pl.pallas_call(kernel, out_shape=[jax.ShapeDtypeStruct(left_env.shape, F3...  95.6 us

profile of v9, /device:TPU:5, one launch (start us, length us, event | category | flops | bytes accessed | tf_op | source)
XLA Modules:
  0.0 98.1 jit_solution(12408475729290296160)
XLA Ops:
  0.6 95.6 %shard_map.77 = (f32[1,32,16,512]{3,2,1,0:T(8,128)S(1)}, f32[1,32,16,512]{3,2,1,0:T(8,128)S(1)}) custom-call(f32[1,32,16,512]{3,2,1,0:T(8,128)} %le.1, f32[1,32,16,512]{3,2,1,0:T(8,128)} %re.1, f32[1,512,4,512]{3,2,1,0:T(4,128)} %ls.1, f32[1,512,4,512]{3,2,1,0:T(4,128)} %rs.1, f32[16,4,4,16]{3,2,1,0:T(4,128)} %bitcast.6, f32[16,4,4,16]{3,2,1,0:T(4,128)} %bitcast.7), custom_call_target="tpu_custom_call" | custom-call | tf_op jit(solution)/shard_map/pallas_call | solution.py:487
  96.2 1.0 copy.10
  97.2 1.0 copy.11
